TPU v7x, 512 devices: a whole 4x4x16 slice. The times are simulated.
512 devices in a mesh: blk: 128 (over z, x, core), sub: 4 (over y).
Axes of the slice: x: 4, y: 4, z: 16, core: 2. Of those that a mesh axis runs over, the one named last changes fastest.
Arguments:
- features: bfloat16 [16, 1048576], P(None, ('blk', 'sub')), may hold values from -6 to 6
- adjacency: bfloat16 [8192, 8, 128, 128], P(('blk', 'sub')), may hold values from 0.049804688 to 2
- col_tiles: int32 [8192, 8], P(('blk', 'sub')), may hold values from 0 to 8191, as said below
- match_one: int32 [4096, 128], replicated, may hold values from 0 to 127, each once within a row
- match_two: int32 [2048, 128], replicated, may hold values from 0 to 127, each once within a row
Outputs:
- coarse_adjacency: bfloat16 [2048, 8, 128, 128], P(('blk', 'sub'))
- coarse_features: bfloat16 [16, 262144], P(None, ('blk', 'sub'))
Inputs may be any that keep to these rules, and one draw needn't show every extreme that they name: `col_tiles`: for each slot k, the two tiles t and t + 64 of a level-one pair ((t // 64) even) name column tiles that differ by 0 or 64; with that difference cleared, the tiles t and t + 16 ((t // 16) even, (t // 64) even) name column tiles that differ by 0 or 16. `match_one`: each row is a matching of the high tile's rows onto the low tile's rows. `match_two`: each row is a matching of the high tile's rows onto the low tile's rows.
All inputs are finite; a program needn't handle non-finite values.
Results may differ from a plain program's by a relative error of at most 0.0053.
Values may be sent and summed in bfloat16 or wider, within the bound.
A program may use at most 64 MiB of HBM per device.

v0:
```python
import jax
import jax.numpy as jnp
from jax import lax
from jax.sharding import PartitionSpec as P


def swapped(value, axis, stride):
    mask = 2**stride
    pairs = [(source, source ^ mask) for source in range(lax.axis_size(axis))]
    return lax.ppermute(value, axis, pairs)


def one_hot(row_maps, positions):
    return (row_maps[..., :, None] == positions).astype(jnp.bfloat16)


def pair_of(column_ids, block_span):
    return column_ids // (2 * block_span) * block_span + column_ids % block_span


def first_maps(column_ids, match_one, block_span, positions):
    upper = column_ids // block_span % 2 == 1
    return jnp.where(upper[..., None], match_one[pair_of(column_ids, block_span)], positions)


def second_maps(column_ids, match_two, block_span, tile_count, positions):
    pair_index = pair_of(column_ids, block_span)
    group_index = pair_index // (2 * tile_count) * tile_count + pair_index % tile_count
    upper = column_ids // tile_count % 2 == 1
    return jnp.where(upper[..., None], match_two[group_index], positions)


def column_side(blocks, row_maps, positions):
    hot = one_hot(row_maps, positions)
    return jnp.einsum("jkab,jkbc->jkac", blocks, hot, preferred_element_type=jnp.float32).astype(
        jnp.bfloat16
    )


def row_side(row_hot, blocks):
    return jnp.einsum("jba,jkbc->jkac", row_hot, blocks, preferred_element_type=jnp.float32)


def feature_side(feats, row_hot):
    return jnp.einsum("fjb,jba->fja", feats, row_hot, preferred_element_type=jnp.float32)


def add_pair(first_part, second_part):
    return (first_part.astype(jnp.float32) + second_part.astype(jnp.float32)).astype(jnp.bfloat16)


def per_device(features, adjacency, col_tiles, match_one, match_two):
    tile_count = adjacency.shape[0]
    slot_count = adjacency.shape[1]
    tile_width = adjacency.shape[2]
    feat_count = features.shape[0]
    quarter = tile_count // 4
    sub_count = lax.axis_size("sub")
    block_span = sub_count * tile_count
    blk_index = lax.axis_index("blk")
    sub_index = lax.axis_index("sub")
    positions = jnp.arange(tile_width, dtype=jnp.int32)
    feats = features.reshape(feat_count, tile_count, tile_width)
    own_cols = column_side(
        adjacency, first_maps(col_tiles, match_one, block_span, positions), positions
    )
    first_pair = (blk_index // 2 * sub_count + sub_index) * tile_count
    rows_one = one_hot(lax.dynamic_slice_in_dim(match_one, first_pair, tile_count, 0), positions)
    first_group = (blk_index // 2 * (sub_count // 2) + sub_index // 2) * tile_count
    high_one = blk_index % 2 == 1
    high_two = sub_index % 2 == 1
    blk_even = blk_index % 2 == 0
    sub_even = sub_index % 2 == 0
    terms_tiles, terms_feats = lax.cond(
        high_one,
        lambda: (
            row_side(rows_one, own_cols).astype(jnp.bfloat16),
            feature_side(feats, rows_one).astype(jnp.bfloat16),
        ),
        lambda: (own_cols, feats),
    )
    grid_tiles = terms_tiles.reshape(quarter, 2, 2, slot_count, tile_width, tile_width)
    grid_feats = terms_feats.reshape(feat_count, quarter, 2, 2, tile_width)
    keep_tiles = jnp.where(blk_even, grid_tiles[:, 0], grid_tiles[:, 1])
    send_tiles = jnp.where(blk_even, grid_tiles[:, 1], grid_tiles[:, 0])
    keep_feats = jnp.where(blk_even, grid_feats[:, :, 0], grid_feats[:, :, 1])
    send_feats = jnp.where(blk_even, grid_feats[:, :, 1], grid_feats[:, :, 0])
    got_tiles, got_feats = swapped((send_tiles, send_feats), "blk", 0)
    level_tiles = add_pair(keep_tiles, got_tiles).reshape(
        2 * quarter, slot_count, tile_width, tile_width
    )
    level_feats = add_pair(keep_feats, got_feats).reshape(feat_count, 2 * quarter, tile_width)
    level_cols = col_tiles - col_tiles // block_span % 2 * block_span
    grid_cols = level_cols.reshape(quarter, 2, 2, slot_count)
    keep_cols = jnp.where(blk_even, grid_cols[:, 0], grid_cols[:, 1]).reshape(
        2 * quarter, slot_count
    )
    own_two = column_side(
        level_tiles, second_maps(keep_cols, match_two, block_span, tile_count, positions), positions
    )
    all_rows = one_hot(lax.dynamic_slice_in_dim(match_two, first_group, tile_count, 0), positions)
    grid_rows = all_rows.reshape(quarter, 2, 2, tile_width, tile_width)
    rows_two = jnp.where(blk_even, grid_rows[:, 0], grid_rows[:, 1]).reshape(
        2 * quarter, tile_width, tile_width
    )
    second_tiles, second_feats = lax.cond(
        high_two,
        lambda: (
            row_side(rows_two, own_two).astype(jnp.bfloat16),
            feature_side(level_feats, rows_two).astype(jnp.bfloat16),
        ),
        lambda: (own_two, level_feats),
    )
    grid_two = second_tiles.reshape(quarter, 2, slot_count, tile_width, tile_width)
    grid_feats_two = second_feats.reshape(feat_count, quarter, 2, tile_width)
    keep_two = jnp.where(sub_even, grid_two[:, 0], grid_two[:, 1])
    send_two = jnp.where(sub_even, grid_two[:, 1], grid_two[:, 0])
    keep_feats_two = jnp.where(sub_even, grid_feats_two[:, :, 0], grid_feats_two[:, :, 1])
    send_feats_two = jnp.where(sub_even, grid_feats_two[:, :, 1], grid_feats_two[:, :, 0])
    got_two, got_feats_two = swapped((send_two, send_feats_two), "sub", 0)
    final_tiles = add_pair(keep_two, got_two)
    final_feats = add_pair(keep_feats_two, got_feats_two)
    return (final_tiles, final_feats.reshape(feat_count, quarter * tile_width))


def solution(mesh):
    placed = (
        P(None, ("blk", "sub")),
        P(("blk", "sub"), None, None, None),
        P(("blk", "sub"), None),
        P(),
        P(),
    )
    return jax.shard_map(
        per_device,
        mesh=mesh,
        in_specs=placed,
        out_specs=(P(("blk", "sub"), None, None, None), P(None, ("blk", "sub"))),
        check_vma=False,
    )
```

profile of v0, /device:TPU:1, one launch (start us, length us, event | category | flops | bytes accessed | tf_op | source)
XLA Modules:
  0.0 83.3 jit_solution(14519965595498528917)
XLA Ops:
  0.7 0.9 %copy.37 = s32[16,8]{1,0:T(8,128)S(1)} copy(s32[16,8]{0,1:T(8,128)} %param.11) | data formatting | bytes 1024 | tf_op args[2]
  1.6 0.6 copy-done
  2.2 0.3 fusion.7
  2.7 0.6 gather_fusion
  3.3 0.8 %copy.62 = bf16[2,8,16,128]{3,2,1,0:T(8,128)(2,1)S(1)} copy(bf16[2,8,16,128]{3,1,2,0:T(8,128)(2,1)} %bitcast.118) | data formatting | bytes 131072
  4.3 7.2 %convert_bitcast_fusion = bf16[16,8,128,128]{2,3,1,0:T(8,128)(2,1)} fusion(bf16[16,8,128,128]{3,2,1,0:T(8,128)(2,1)} %param.10, s32[16,8,128]{2,1,0:T(8,128)S(1)} %bitcast_select_fusion), kind=kOutput, calls=%fused_computation.29 | convolution fusion | flops 541065216 | bytes 8454144 | tf_op jit(solution)/shard_map/jkab,jkbc->jkac/dot_general | solution.py:35
  11.4 6.0 %conditional.2 = (bf16[4,2,8,128,128]{3,4,2,1,0:T(8,128)(2,1)}, bf16[4,2,8,128,128]{3,4,2,1,0:T(8,128)(2,1)}, bf16[16,4,2,128]{3,0,2,1:T(8,128)(2,1)S(1)}, bf16[16,4,2,128]{3,0,2,1:T(8,128)(2,1)S(1)}) conditional(s32[]{:T(128)} %convert_element_type.89, (bf16[16,8,128,128]{2,3,1,0:T(8,128)(2,1)}, bf16[16,16,128]{2,1,0:T(8,128)(2,1)S(1)}) %tuple.64, ...), branch_computations={%region_0.1_spmd, %region_1.2_spmd} | conditional | flops 547389440 | bytes 25428000 | solution.py:74
  11.4 3.4 %convolution_convert_fusion = bf16[16,8,128,128]{3,2,1,0:T(8,128)(2,1)S(1)} fusion(bf16[16,8,128,128]{2,3,1,0:T(8,128)(2,1)} %get-tuple-element.83, bf16[16,128,128]{2,1,0:T(8,128)(2,1)S(1)} %get-tuple-element.84), kind=kOutput, calls=%fused_computation.6 | convolution fusion | flops 538968064 | bytes 8912896 | tf_op jit(solution)/shard_map/cond/branch_1_fun/jba,jkbc->jkac/dot_general | solution.py:41
  14.9 2.3 %slice_bitcast_fusion.4 = (bf16[4,2,8,128,128]{3,4,2,1,0:T(8,128)(2,1)}, bf16[4,2,8,128,128]{3,4,2,1,0:T(8,128)(2,1)}) fusion(bf16[4,2,2,8,128,128]{4,5,3,2,1,0:T(8,128)(2,1)S(1)} %bitcast.105), kind=kLoop, calls=%fused_computation.7 | loop fusion | bytes 8388608 | tf_op jit(solution)/shard_map/squeeze | solution.py:84
  17.2 0.2 convolution_convert_fusion.1
  17.4 3.1 %broadcast_select_fusion = bf16[4,2,8,128,128]{3,4,2,1,0:T(8,128)(2,1)} fusion(bf16[4,2,8,128,128]{3,4,2,1,0:T(8,128)(2,1)} %get-tuple-element.103, bf16[4,2,8,128,128]{3,4,2,1,0:T(8,128)(2,1)} %get-tuple-element.102, pred[]{:T(512)} %eq.94), kind=kLoop, calls=%fused_computation.34 | loop fusion | flops 1048576 | bytes 6291457 | tf_op jit(solution)/shard_map/jit(_where)/select_n | solution.py:85
  20.6 22.0 %collective-permute-start = (bf16[4,2,8,128,128]{3,4,2,1,0:T(8,128)(2,1)}, bf16[4,2,8,128,128]{3,4,2,1,0:T(8,128)(2,1)}, u32[]{:S(2)}, u32[]{:S(2)}) collective-permute-start(bf16[4,2,8,128,128]{3,4,2,1,0:T(8,128)(2,1)} %broadcast_select_fusion), channel_id=1, source_target_pairs={{0,4},{4,0},{8,12},{12,8},{16,20},{20,16},{24,28},{28,24},{32,36},... | collective-permute-start | bytes 6291464 | tf_op jit(solution)/shard_map/ppermute | solution.py:10
  42.6 1.9 %collective-permute-start.1 = (bf16[16,4,2,128]{3,0,2,1:T(8,128)(2,1)S(1)}, bf16[16,4,2,128]{3,0,2,1:T(8,128)(2,1)S(1)}, u32[]{:S(2)}, u32[]{:S(2)}) collective-permute-start(bf16[16,4,2,128]{3,0,2,1:T(8,128)(2,1)S(1)} %broadcast_select_fusion.2), channel_id=1, source_target_pairs={{0,4},{4,0},{8,12},{12,8},{16,20},{20,16},{24,28},{28,24},{32,36},... | collective-permute-start | bytes 98312 | tf_op jit(solution)/shard_map/ppermute | solution.py:10
  44.6 1.8 %gather_fusion.1 = s32[64,128]{1,0:T(8,128)S(1)} fusion(s32[2048,128]{1,0:T(8,128)} %param.13, s32[1024]{0:T(1024)S(1)} %pad_clamp_fusion), kind=kCustom, calls=%fused_computation.1 | custom fusion | bytes 65792 | tf_op jit(solution)/shard_map/gather | solution.py:30
  46.5 0.7 constant_dynamic-slice_fusion
  47.2 1.1 %fusion.8 = bf16[4,2,2,128,128]{4,3,2,0,1:T(8,128)(2,1)} fusion(s32[4,2,2,128]{3,2,1,0:T(2,128)S(1)} %bitcast.121), kind=kLoop, calls=%fused_computation.39 | loop fusion | flops 524288 | bytes 532480 | tf_op jit(solution)/shard_map/convert_element_type | solution.py:14
  48.4 3.4 %add_convert_fusion = bf16[4,2,8,128,128]{3,4,2,1,0:T(8,128)(2,1)S(1)} fusion(bf16[4,2,8,128,128]{3,4,2,1,0:T(8,128)(2,1)} %collective-permute-done, bf16[4,2,8,128,128]{3,4,2,1,0:T(8,128)(2,1)} %get-tuple-element.102, bf16[4,2,8,128,128]{3,4,2,1,0:T(8,128)(2,1)} %get-tuple-element.103, pred[]{:T(512)} %eq.94), kind=kLoop, calls=%fused_computation.28 | loop fusion | flops 5242880 | bytes 8388609 | tf_op jit(solution)/shard_map/convert_element_type | solution.py:49
  51.9 2.6 %fusion.6 = bf16[8,8,128,128]{3,2,1,0:T(8,128)(2,1)S(1)} fusion(bf16[8,8,128,128]{2,3,1,0:T(8,128)(2,1)S(1)} %bitcast.107, s32[8,8,128]{2,1,0:T(8,128)S(1)} %bitcast_select_fusion.1), kind=kOutput, calls=%fused_computation.35 | convolution fusion | flops 270532608 | bytes 4227072 | tf_op jit(solution)/shard_map/jkab,jkbc->jkac/dot_general | solution.py:35
  54.4 0.2 conditional.3
  54.8 1.9 %collective-permute-start.2 = (bf16[4,8,128,128]{3,2,1,0:T(8,128)(2,1)S(1)}, bf16[4,8,128,128]{3,2,1,0:T(8,128)(2,1)S(1)}, u32[]{:S(2)}, u32[]{:S(2)}) collective-permute-start(bf16[4,8,128,128]{3,2,1,0:T(8,128)(2,1)S(1)} %broadcast_select_fusion.1), channel_id=1, source_target_pairs={{0,1},{1,0},{2,3},{3,2},{4,5},{5,4},{6,7},{7,6},{8,9},{9,8},{10,11... | collective-permute-start | bytes 3145736 | tf_op jit(solution)/shard_map/ppermute | solution.py:10
  56.7 3.4 %collective-permute-start.3 = (bf16[16,4,128]{2,0,1:T(8,128)(2,1)S(1)}, bf16[16,4,128]{2,0,1:T(8,128)(2,1)S(1)}, u32[]{:S(2)}, u32[]{:S(2)}) collective-permute-start(bf16[16,4,128]{2,0,1:T(8,128)(2,1)S(1)} %broadcast_select_fusion.3), channel_id=1, source_target_pairs={{0,1},{1,0},{2,3},{3,2},{4,5},{5,4},{6,7},{7,6},{8,9},{9,8},{10,11... | collective-permute-start | bytes 49160 | tf_op jit(solution)/shard_map/ppermute | solution.py:10
  60.1 21.2 %collective-permute-done.3 = bf16[16,4,128]{2,0,1:T(8,128)(2,1)S(1)} collective-permute-done((bf16[16,4,128]{2,0,1:T(8,128)(2,1)S(1)}, bf16[16,4,128]{2,0,1:T(8,128)(2,1)S(1)}, u32[]{:S(2)}, u32[]{:S(2)}) %collective-permute-start.3) | collective-permute-done | bytes 16416 | tf_op jit(solution)/shard_map/ppermute | solution.py:10
  81.2 0.6 copy_bitcast_fusion
  81.8 1.5 %add_convert_fusion.1 = bf16[4,8,128,128]{3,2,1,0:T(8,128)(2,1)} fusion(bf16[4,8,128,128]{3,2,1,0:T(8,128)(2,1)S(1)} %collective-permute-done.2, bf16[4,8,128,128]{3,2,1,0:T(8,128)(2,1)S(1)} %get-tuple-element.106, bf16[4,8,128,128]{3,2,1,0:T(8,128)(2,1)S(1)} %get-tuple-element.107, pred[]{:T(512)S(6)} %eq.92), kind=kLoop, calls=%fused_computation.32 | loop fusion | flops 2621440 | bytes 4194305 | tf_op jit(solution)/shard_map/convert_element_type | solution.py:49
  (25 shorter events, 0.8 us)
Async XLA Ops:
  0.6 1.6 %copy-start = (s32[4096,128]{1,0:T(8,128)S(1)}, s32[4096,128]{1,0:T(8,128)}, u32[]{:S(2)}) copy-start(s32[4096,128]{1,0:T(8,128)} %param.12) | copy-start | bytes 6291460
  20.6 27.9 %collective-permute-start = (bf16[4,2,8,128,128]{3,4,2,1,0:T(8,128)(2,1)}, bf16[4,2,8,128,128]{3,4,2,1,0:T(8,128)(2,1)}, u32[]{:S(2)}, u32[]{:S(2)}) collective-permute-start(bf16[4,2,8,128,128]{3,4,2,1,0:T(8,128)(2,1)} %broadcast_select_fusion), channel_id=1, source_target_pairs={{0,4},{4,0},{8,12},{12,8},{16,20},{20,16},{24,28},{28,24},{32,36},... | collective-permute-start | bytes 6291464 | tf_op jit(solution)/shard_map/ppermute | solution.py:10
  42.6 5.8 %collective-permute-start.1 = (bf16[16,4,2,128]{3,0,2,1:T(8,128)(2,1)S(1)}, bf16[16,4,2,128]{3,0,2,1:T(8,128)(2,1)S(1)}, u32[]{:S(2)}, u32[]{:S(2)}) collective-permute-start(bf16[16,4,2,128]{3,0,2,1:T(8,128)(2,1)S(1)} %broadcast_select_fusion.2), channel_id=1, source_target_pairs={{0,4},{4,0},{8,12},{12,8},{16,20},{20,16},{24,28},{28,24},{32,36},... | collective-permute-start | bytes 98312 | tf_op jit(solution)/shard_map/ppermute | solution.py:10
  51.8 2.6 %copy-start.1 = (bf16[4,2,2,128,128]{4,3,2,0,1:T(8,128)(2,1)S(1)}, bf16[4,2,2,128,128]{4,3,2,0,1:T(8,128)(2,1)}, u32[]{:S(2)}) copy-start(bf16[4,2,2,128,128]{4,3,2,0,1:T(8,128)(2,1)} %fusion.8) | copy-start | bytes 1572868
  54.8 27.1 %collective-permute-start.2 = (bf16[4,8,128,128]{3,2,1,0:T(8,128)(2,1)S(1)}, bf16[4,8,128,128]{3,2,1,0:T(8,128)(2,1)S(1)}, u32[]{:S(2)}, u32[]{:S(2)}) collective-permute-start(bf16[4,8,128,128]{3,2,1,0:T(8,128)(2,1)S(1)} %broadcast_select_fusion.1), channel_id=1, source_target_pairs={{0,1},{1,0},{2,3},{3,2},{4,5},{5,4},{6,7},{7,6},{8,9},{9,8},{10,11... | collective-permute-start | bytes 3145736 | tf_op jit(solution)/shard_map/ppermute | solution.py:10
  56.7 24.5 %collective-permute-start.3 = (bf16[16,4,128]{2,0,1:T(8,128)(2,1)S(1)}, bf16[16,4,128]{2,0,1:T(8,128)(2,1)S(1)}, u32[]{:S(2)}, u32[]{:S(2)}) collective-permute-start(bf16[16,4,128]{2,0,1:T(8,128)(2,1)S(1)} %broadcast_select_fusion.3), channel_id=1, source_target_pairs={{0,1},{1,0},{2,3},{3,2},{4,5},{5,4},{6,7},{7,6},{8,9},{9,8},{10,11... | collective-permute-start | bytes 49160 | tf_op jit(solution)/shard_map/ppermute | solution.py:10
where the time goes:
time: 84 us; the launch traced here: 83.3 us
  starting transfers between devices  29.2 us (35%)
  waiting for transfers between devices  21.2 us (25%)
  matrix products  13.4 us (16%)
  other arithmetic  10.5 us (12%)
  local copies, waits for them, and re-layouts  8.16 us (10%)
  between operations  0.86 us (1%)
    ppermute x4, starting transfers between devices, swapped(): return lax.ppermute(value, axis, pairs)  29.2 us
    ppermute x4, waiting for transfers between devices, swapped(): return lax.ppermute(value, axis, pairs)  21.2 us
    dot_general x2, matrix products, column_side(): jnp.einsum('jkab,jkbc->jkac', blocks, hot, preferred_element_type=jnp.flo...  9.71 us
    convert_element_type x3, other arithmetic, add_pair(): (first_part.astype(jnp.float32) + second_part.astype(jnp.float32)).astype...  4.88 us
    dot_general x1, matrix products, row_side(): jnp.einsum('jba,jkbc->jkac', row_hot, blocks, preferred_element_type=jnp....  3.42 us
    select_n x1, other arithmetic, per_device(): send_tiles = jnp.where(blk_even, grid_tiles[:, 1], grid_tiles[:, 0])  3.13 us
    unnamed x6, local copies, waits for them, and re-layouts  2.36 us
    squeeze x1, local copies, waits for them, and re-layouts, per_device(): keep_tiles = jnp.where(blk_even, grid_tiles[:, 0], grid_tiles[:, 1])  2.3 us
  transfers between devices with their start and end apart: 4, of which 1 were waited for; matrix products, arithmetic and copies ran while one was open for 5% of the time, Pallas kernels for 0%

commit v1 on v0

v1 whole, which is shorter than its diff:
```python
import functools

import jax
import jax.numpy as jnp
from jax import lax
from jax.experimental import pallas as pl
from jax.experimental.pallas import tpu as pltpu
from jax.sharding import PartitionSpec as P

MESH = pl.DeviceIdType.MESH
GROUP = 2


def turned(row_map, width):
    down = lax.broadcasted_iota(jnp.int32, (width, width), 0)
    return jnp.where(down == row_map, 1.0, 0.0).astype(jnp.bfloat16)


def right_side(blocks, turned_hot):
    return lax.dot_general(
        blocks, turned_hot, (((1,), (1,)), ((), ())), preferred_element_type=jnp.float32
    )


def merged(low, high, turned_rows, turned_cols):
    width = turned_rows.shape[0]
    moved = jnp.dot(
        turned_rows, jnp.concatenate(high, axis=1), preferred_element_type=jnp.float32
    ).astype(jnp.bfloat16)
    out = []
    for n, block in enumerate(low):
        both = jnp.concatenate([block, moved[:, n * width : (n + 1) * width]], axis=1)
        out.append(right_side(both, turned_cols[n]).astype(jnp.bfloat16))
    return out


def kernel(
    span, feat, adj, cols, m1, m2, out_a, out_f,
    m1v, m2v, col_s, col_1, col_2, adj_v, feat_v, send_a, send_f, lev_a, lev_f, fin_a, fin_f,
    loc_sem, own_sem, put_sem, cs_sem, cr_sem, ss_sem, sr_sem, xs_sem, xr_sem,
):
    tiles, slots, width = adj.shape[0], adj.shape[1], adj.shape[2]
    quarter = tiles // 4
    groups = slots // GROUP
    blk, sub = lax.axis_index("blk"), lax.axis_index("sub")
    b, s = lax.rem(blk, 2), lax.rem(sub, 2)
    core = {"blk": blk + 1 - 2 * b}
    near = {"sub": sub + 1 - 2 * s}
    subs = span // tiles
    first_pair = (blk // 2 * subs + sub) * tiles
    first_group = (blk // 2 * (subs // 2) + sub // 2) * tiles
    lanes = lax.broadcasted_iota(jnp.int32, (1, width), 1)

    def side(j):
        return (1 - s) * (1 - j) + s * j

    def own_copy(j, i, q):
        part = pl.ds(q * GROUP, GROUP)
        return pltpu.make_async_copy(
            adj.at[4 * i + 2 * b + side(j), part], adj_v.at[b, j, i, part], own_sem.at[j, i, q]
        )

    def core_copy(j, i, q):
        part = pl.ds(q * GROUP, GROUP)
        return pltpu.make_async_remote_copy(
            src_ref=adj.at[4 * i + 2 * (1 - b) + side(j), part],
            dst_ref=adj_v.at[b, j, i, part],
            send_sem=cs_sem.at[j, i, q], recv_sem=cr_sem.at[j, i, q],
            device_id=core, device_id_type=MESH,
        )

    def sub_copy(i, q):
        part = pl.ds(q * GROUP, GROUP)
        return pltpu.make_async_remote_copy(
            src_ref=send_a.at[i, part], dst_ref=lev_a.at[s, i, part],
            send_sem=ss_sem.at[i, q], recv_sem=sr_sem.at[i, q],
            device_id=near, device_id_type=MESH,
        )

    def small(src, dst, n, device):
        return pltpu.make_async_remote_copy(
            src_ref=src, dst_ref=dst, send_sem=xs_sem.at[n], recv_sem=xr_sem.at[n],
            device_id=device, device_id_type=MESH,
        )

    def put_copy(i, q):
        part = pl.ds(q * GROUP, GROUP)
        return pltpu.make_async_copy(fin_a.at[i, part], out_a.at[i, part], put_sem.at[i, q])

    barrier = pltpu.get_barrier_semaphore()
    pl.semaphore_signal(barrier, inc=1, device_id=core, device_id_type=MESH)
    pl.semaphore_signal(barrier, inc=1, device_id=near, device_id_type=MESH)

    local = [
        pltpu.make_async_copy(cols, col_s, loc_sem.at[0]),
        pltpu.make_async_copy(cols, col_1.at[b], loc_sem.at[1]),
        pltpu.make_async_copy(cols, col_2.at[s], loc_sem.at[2]),
        pltpu.make_async_copy(m1, m1v, loc_sem.at[3]),
        pltpu.make_async_copy(feat, feat_v.at[b], loc_sem.at[4]),
        pltpu.make_async_copy(m2, m2v, loc_sem.at[5]),
    ]
    for n in range(4):
        local[n].start()
    for q in range(groups):
        own_copy(0, 0, q).start()

    pl.semaphore_wait(barrier, 2)
    cols_core = small(cols, col_1.at[b], 0, core)
    cols_near = small(cols, col_2.at[s], 1, near)
    feat_core = small(feat, feat_v.at[b], 2, core)
    cols_core.start()
    for q in range(groups):
        core_copy(0, 0, q).start()
    cols_near.start()
    feat_core.start()
    local[4].start()

    @pl.loop(1, quarter)
    def _(i):
        for q in range(groups):
            core_copy(0, i, q).start()
            own_copy(0, i, q).start()

    @pl.loop(0, quarter)
    def _(i):
        for q in range(groups):
            core_copy(1, i, q).start()
            own_copy(1, i, q).start()

    local[5].start()

    for n in range(4):
        local[n].wait()
    cols_core.wait()

    def columns(table, maps, tile, k, bit, row):
        here = maps[pl.ds(row, 1), :]
        hots = []
        for part in range(2):
            flags = table[part, pl.ds(tile, 1), :][:, k : k + 1]
            hots.append(turned(jnp.where((flags & bit) != 0, here, lanes), width))
        return jnp.concatenate(hots, axis=1)

    def first_level(j, i, store):
        tile = 4 * i + 2 * b + side(j)
        rows = turned(m1v[pl.ds(first_pair + tile, 1), :], width)
        for q in range(groups):
            own_copy(j, i, q).wait()
            core_copy(j, i, q).wait_recv()
            ks = range(q * GROUP, (q + 1) * GROUP)
            hots = []
            for k in ks:
                c = col_s[tile, k]
                hots.append(
                    columns(col_1, m1v, tile, k, span, c // (2 * span) * span + lax.rem(c, span))
                )
            done = merged(
                [adj_v[0, j, i, k] for k in ks], [adj_v[1, j, i, k] for k in ks], rows, hots
            )
            store(i, q, ks, done)
        return tile, rows

    def feature_level(j, i, tile, rows, dst):
        at = pl.ds(pl.multiple_of(tile * width, width), width)
        total = feat_v[0, :, at].astype(jnp.float32) + right_side(feat_v[1, :, at], rows)
        dst[:, pl.ds(pl.multiple_of(i * width, width), width)] = total.astype(jnp.bfloat16)

    def store_send(i, q, ks, done):
        for k, block in zip(ks, done):
            send_a[i, k] = block
        sub_copy(i, q).start()

    def store_keep(i, q, ks, done):
        for k, block in zip(ks, done):
            lev_a[s, i, k] = block

    @pl.loop(0, quarter)
    def _(i):
        first_level(0, i, store_send)

    local[4].wait()
    feat_core.wait()

    @pl.loop(0, quarter)
    def _(i):
        tile = 4 * i + 2 * b + side(0)
        rows = turned(m1v[pl.ds(first_pair + tile, 1), :], width)
        feature_level(0, i, tile, rows, send_f)

    feat_near = small(send_f, lev_f.at[s], 3, near)
    feat_near.start()

    @pl.loop(0, quarter)
    def _(i):
        tile, rows = first_level(1, i, store_keep)
        feature_level(1, i, tile, rows, lev_f.at[s])

    local[5].wait()
    cols_near.wait()

    @pl.loop(0, quarter)
    def _(i):
        tile = 4 * i + 2 * b + s
        rows = turned(m2v[pl.ds(first_group + tile, 1), :], width)
        for q in range(groups):
            sub_copy(i, q).wait_recv()
            ks = range(q * GROUP, (q + 1) * GROUP)
            hots = []
            for k in ks:
                c = col_s[tile, k]
                p = c // (2 * span) * span + lax.rem(c, span)
                hots.append(
                    columns(col_2, m2v, tile, k, tiles, p // (2 * tiles) * tiles + lax.rem(p, tiles))
                )
            done = merged([lev_a[0, i, k] for k in ks], [lev_a[1, i, k] for k in ks], rows, hots)
            for k, block in zip(ks, done):
                fin_a[i, k] = block
            put_copy(i, q).start()

    feat_near.wait()
    for i in range(quarter):
        tile = 4 * i + 2 * b + s
        rows = turned(m2v[pl.ds(first_group + tile, 1), :], width)
        at = pl.ds(i * width, width)
        total = lev_f[0, :, at].astype(jnp.float32) + right_side(lev_f[1, :, at], rows)
        fin_f[:, at] = total.astype(jnp.bfloat16)
    put_f = pltpu.make_async_copy(fin_f, out_f, loc_sem.at[6])
    put_f.start()

    @pl.loop(0, quarter)
    def _(i):
        for q in range(groups):
            core_copy(0, i, q).wait_send()
            core_copy(1, i, q).wait_send()
            sub_copy(i, q).wait_send()
            put_copy(i, q).wait()

    put_f.wait()


def per_device(features, adjacency, col_tiles, match_one, match_two):
    tiles, slots, width = adjacency.shape[:3]
    feats = features.shape[0]
    quarter, groups = tiles // 4, slots // GROUP
    span = lax.axis_size("sub") * tiles
    half = jnp.bfloat16
    dma = pltpu.SemaphoreType.DMA
    anywhere = pl.BlockSpec(memory_space=pl.ANY)
    return pl.pallas_call(
        functools.partial(kernel, span),
        out_shape=(
            jax.ShapeDtypeStruct((quarter, slots, width, width), half),
            jax.ShapeDtypeStruct((feats, quarter * width), half),
        ),
        in_specs=[anywhere] * 5,
        out_specs=(anywhere, anywhere),
        scratch_shapes=[
            pltpu.VMEM(match_one.shape, jnp.int32),
            pltpu.VMEM(match_two.shape, jnp.int32),
            pltpu.SMEM(col_tiles.shape, jnp.int32),
            pltpu.VMEM((2,) + col_tiles.shape, jnp.int32),
            pltpu.VMEM((2,) + col_tiles.shape, jnp.int32),
            pltpu.VMEM((2, 2, quarter, slots, width, width), half),
            pltpu.VMEM((2,) + features.shape, half),
            pltpu.VMEM((quarter, slots, width, width), half),
            pltpu.VMEM((feats, quarter * width), half),
            pltpu.VMEM((2, quarter, slots, width, width), half),
            pltpu.VMEM((2, feats, quarter * width), half),
            pltpu.VMEM((quarter, slots, width, width), half),
            pltpu.VMEM((feats, quarter * width), half),
            dma((7,)),
            dma((2, quarter, groups)),
            dma((quarter, groups)),
            dma((2, quarter, groups)),
            dma((2, quarter, groups)),
            dma((quarter, groups)),
            dma((quarter, groups)),
            dma((4,)),
            dma((4,)),
        ],
        compiler_params=pltpu.CompilerParams(collective_id=0, has_side_effects=True),
        name="coarsen",
    )(features, adjacency, col_tiles, match_one, match_two)


def solution(mesh):
    placed = (
        P(None, ("blk", "sub")),
        P(("blk", "sub"), None, None, None),
        P(("blk", "sub"), None),
        P(),
        P(),
    )
    return jax.shard_map(
        per_device,
        mesh=mesh,
        in_specs=placed,
        out_specs=(P(("blk", "sub"), None, None, None), P(None, ("blk", "sub"))),
        check_vma=False,
    )
```

time: 84 us -> 42.5 us (0.51)
  Pallas kernels: 0 us -> 36.6 us
  starting transfers between devices: 29.2 us -> 0 us
  waiting for transfers between devices: 21.2 us -> 0 us
  matrix products: 13.4 us -> 0 us
  other arithmetic: 10.5 us -> 0 us
  local copies, waits for them, and re-layouts: 8.16 us -> 4.99 us
    pallas_call x0 -> x1, Pallas kernels: none -> 36.6 us  [per_device(): pl.pallas_call(functools.partial(kernel, span), out_shape=(jax.ShapeDtype...]
    ppermute x4 -> x0, starting transfers between devices: 29.2 us -> none  [swapped(): return lax.ppermute(value, axis, pairs)]
    ppermute x4 -> x0, waiting for transfers between devices: 21.2 us -> none  [swapped(): return lax.ppermute(value, axis, pairs)]
    dot_general x4 -> x0, matrix products: 13.4 us -> none  [the longest x2 9.71 us: column_side(): jnp.einsum('jkab,jkbc->jkac', blocks, hot, preferred_element_type=jnp.flo...]
    convert_element_type x5 -> x0, other arithmetic: 6.36 us -> none  [the longest x3 4.88 us: add_pair(): (first_part.astype(jnp.float32) + second_part.astype(jnp.float32)).astype...]
    select_n x8 -> x0, other arithmetic: 3.47 us -> none  [the longest x1 3.13 us: per_device(): send_tiles = jnp.where(blk_even, grid_tiles[:, 1], grid_tiles[:, 0])]
    unnamed x6 -> x3, local copies, waits for them, and re-layouts: 2.36 us -> 4.99 us
    gather x2 -> x0, local copies, waits for them, and re-layouts: 2.47 us -> none  [the longest x1 1.82 us: second_maps(): return jnp.where(upper[..., None], match_two[group_index], positions)]
  transfers between devices with their start and end apart: 4 -> 0, of which waited for: 1 -> 0; matrix products, arithmetic and copies ran while one was open for 5% -> 0% of each run, Pallas kernels for 0% -> 0%
where the time goes in v1:
time: 42.5 us; the launch traced here: 42.2 us
  Pallas kernels  36.6 us (86%)
  local copies, waits for them, and re-layouts  4.99 us (12%)
  between operations  0.64 us (2%)
    pallas_call x1, Pallas kernels, per_device(): pl.pallas_call(functools.partial(kernel, span), out_shape=(jax.ShapeDtype...  36.6 us
    unnamed x3, local copies, waits for them, and re-layouts  4.99 us

profile of v1, /device:TPU:1, one launch (start us, length us, event | category | flops | bytes accessed | tf_op | source)
XLA Modules:
  0.0 42.2 jit_solution(3653256172647917613)
XLA Ops:
  0.6 1.4 %copy.7.cols = s32[16,8]{1,0:T(8,128)} copy(s32[16,8]{0,1:T(8,128)} %param.7) | data formatting | bytes 1024 | tf_op args[2]
  2.0 36.6 %coarsen.1 = (bf16[4,8,128,128]{3,2,1,0:T(8,128)(2,1)}, bf16[16,512]{1,0:T(8,128)(2,1)}) custom-call(bf16[16,2048]{1,0:T(8,128)(2,1)} %feat.1, bf16[16,8,128,128]{3,2,1,0:T(8,128)(2,1)} %adj.1, s32[16,8]{1,0:T(8,128)} %copy.7.cols, s32[4096,128]{1,0:T(8,128)} %m1.1, s32[2048,128]{1,0:T(8,128)} %m2.1), custom_call_target="tpu_custom_call" | custom-call | tf_op jit(solution)/shard_map/coarsen/pallas_call | solution.py:249
  38.6 2.3 %copy.10 = bf16[4,8,128,128]{3,2,1,0:T(8,128)(2,1)} copy(bf16[4,8,128,128]{3,2,1,0:T(8,128)(2,1)} %get-tuple-element.4) | data formatting | bytes 2097152
  40.9 1.3 %copy.11 = bf16[16,512]{1,0:T(8,128)(2,1)} copy(bf16[16,512]{1,0:T(8,128)(2,1)} %get-tuple-element.5) | data formatting | bytes 32768

commit v2 on v1

v2 whole, which is shorter than its diff:
```python
import functools

import jax
import jax.numpy as jnp
from jax import lax
from jax.experimental import pallas as pl
from jax.experimental.pallas import tpu as pltpu
from jax.sharding import PartitionSpec as P

MESH = pl.DeviceIdType.MESH
GROUP = 2
VMEM_BYTES = 24 * 2**20


def turned(row_map, width):
    down = lax.broadcasted_iota(jnp.int32, (width, width), 0)
    return jnp.where(down == row_map, 1.0, 0.0).astype(jnp.bfloat16)


def right_side(blocks, turned_hot):
    return lax.dot_general(
        blocks, turned_hot, (((1,), (1,)), ((), ())), preferred_element_type=jnp.float32
    )


def merged(low, high, turned_rows, turned_cols):
    width = turned_rows.shape[0]
    moved = jnp.dot(
        turned_rows, jnp.concatenate(high, axis=1), preferred_element_type=jnp.float32
    ).astype(jnp.bfloat16)
    out = []
    for n, block in enumerate(low):
        both = jnp.concatenate([block, moved[:, n * width : (n + 1) * width]], axis=1)
        out.append(right_side(both, turned_cols[n]).astype(jnp.bfloat16))
    return out


def kernel(
    span, feat, adj, cols, m1, m2, fin_a, fin_f,
    m1v, m2v, col_1, col_2, adj_v, feat_v, send_a, send_f, lev_a, lev_f,
    loc_sem, own_sem, cs_sem, cr_sem, ss_sem, sr_sem, xs_sem, xr_sem,
):
    tiles, slots, width = adj.shape[0], adj.shape[1], adj.shape[2]
    quarter = tiles // 4
    groups = slots // GROUP
    blk, sub = lax.axis_index("blk"), lax.axis_index("sub")
    b, s = lax.rem(blk, 2), lax.rem(sub, 2)
    core = {"blk": blk + 1 - 2 * b}
    near = {"sub": sub + 1 - 2 * s}
    subs = span // tiles
    first_pair = (blk // 2 * subs + sub) * tiles
    first_group = (blk // 2 * (subs // 2) + sub // 2) * tiles
    pairs, pairs2 = m1.shape[0], m2.shape[0]

    def side(j):
        return (1 - s) * (1 - j) + s * j

    def own_copy(j, i, q):
        part = pl.ds(q * GROUP, GROUP)
        return pltpu.make_async_copy(
            adj.at[4 * i + 2 * b + side(j), part], adj_v.at[b, j, i, part], own_sem.at[j, i, q]
        )

    def core_copy(j, i, q):
        part = pl.ds(q * GROUP, GROUP)
        return pltpu.make_async_remote_copy(
            src_ref=adj.at[4 * i + 2 * (1 - b) + side(j), part],
            dst_ref=adj_v.at[b, j, i, part],
            send_sem=cs_sem.at[j, i, q], recv_sem=cr_sem.at[j, i, q],
            device_id=core, device_id_type=MESH,
        )

    def sub_copy(i, k):
        return pltpu.make_async_remote_copy(
            src_ref=send_a.at[i, k], dst_ref=lev_a.at[s, i, k],
            send_sem=ss_sem.at[i, k], recv_sem=sr_sem.at[i, k],
            device_id=near, device_id_type=MESH,
        )

    def small(src, dst, n, device):
        return pltpu.make_async_remote_copy(
            src_ref=src, dst_ref=dst, send_sem=xs_sem.at[n], recv_sem=xr_sem.at[n],
            device_id=device, device_id_type=MESH,
        )

    barrier = pltpu.get_barrier_semaphore()
    pl.semaphore_signal(barrier, inc=1, device_id=core, device_id_type=MESH)
    pl.semaphore_signal(barrier, inc=1, device_id=near, device_id_type=MESH)

    local = [
        pltpu.make_async_copy(m1, m1v.at[pl.ds(0, pairs)], loc_sem.at[0]),
        pltpu.make_async_copy(cols, col_1.at[b], loc_sem.at[1]),
        pltpu.make_async_copy(cols, col_2.at[s], loc_sem.at[2]),
        pltpu.make_async_copy(feat, feat_v.at[b], loc_sem.at[3]),
        pltpu.make_async_copy(m2, m2v.at[pl.ds(0, pairs2)], loc_sem.at[4]),
    ]
    for n in range(3):
        local[n].start()
    for q in range(groups):
        own_copy(0, 0, q).start()

    plain = lax.broadcasted_iota(jnp.int32, (8, width), 1)
    m1v[pl.ds(pairs, 8), :] = plain
    m2v[pl.ds(pairs2, 8), :] = plain

    pl.semaphore_wait(barrier, 2)
    cols_core = small(cols, col_1.at[b], 0, core)
    cols_near = small(cols, col_2.at[s], 1, near)
    feat_core = small(feat, feat_v.at[b], 2, core)
    cols_core.start()
    for q in range(groups):
        core_copy(0, 0, q).start()
    cols_near.start()
    feat_core.start()
    local[3].start()

    @pl.loop(1, quarter)
    def _(i):
        for q in range(groups):
            core_copy(0, i, q).start()
            own_copy(0, i, q).start()

    @pl.loop(0, quarter)
    def _(i):
        for q in range(groups):
            core_copy(1, i, q).start()
            own_copy(1, i, q).start()

    local[4].start()

    for n in range(3):
        local[n].wait()
    cols_core.wait()

    def columns(table, maps, plain_row, tile, k, bit, row):
        hots = []
        for part in range(2):
            upper = lax.rem(table[part, k, tile] // bit, 2)
            here = maps[pl.ds(upper * row + (1 - upper) * plain_row, 1), :]
            hots.append(turned(here, width))
        return jnp.concatenate(hots, axis=1)

    def first_level(j, i, store):
        tile = 4 * i + 2 * b + side(j)
        rows = turned(m1v[pl.ds(first_pair + tile, 1), :], width)
        for q in range(groups):
            own_copy(j, i, q).wait()
            core_copy(j, i, q).wait_recv()
            ks = range(q * GROUP, (q + 1) * GROUP)
            hots = []
            for k in ks:
                c = col_1[0, k, tile]
                p = c // (2 * span) * span + lax.rem(c, span)
                hots.append(columns(col_1, m1v, pairs, tile, k, span, p))
            done = merged(
                [adj_v[0, j, i, k] for k in ks], [adj_v[1, j, i, k] for k in ks], rows, hots
            )
            store(i, q, ks, done)
        return tile, rows

    def feature_level(j, i, tile, rows, dst):
        at = pl.ds(pl.multiple_of(tile * width, width), width)
        total = feat_v[0, :, at].astype(jnp.float32) + right_side(feat_v[1, :, at], rows)
        dst[:, pl.ds(pl.multiple_of(i * width, width), width)] = total.astype(jnp.bfloat16)

    def store_send(i, q, ks, done):
        for k, block in zip(ks, done):
            send_a[i, k] = block
            sub_copy(i, k).start()

    def store_keep(i, q, ks, done):
        for k, block in zip(ks, done):
            lev_a[s, i, k] = block

    @pl.loop(0, quarter)
    def _(i):
        first_level(0, i, store_send)

    local[3].wait()
    feat_core.wait()

    @pl.loop(0, quarter)
    def _(i):
        tile = 4 * i + 2 * b + side(0)
        rows = turned(m1v[pl.ds(first_pair + tile, 1), :], width)
        feature_level(0, i, tile, rows, send_f)

    feat_near = small(send_f, lev_f.at[s], 3, near)
    feat_near.start()

    @pl.loop(0, quarter)
    def _(i):
        tile, rows = first_level(1, i, store_keep)
        feature_level(1, i, tile, rows, lev_f.at[s])

    local[4].wait()
    cols_near.wait()

    @pl.loop(0, quarter)
    def _(i):
        tile = 4 * i + 2 * b + s
        rows = turned(m2v[pl.ds(first_group + tile, 1), :], width)
        for k in range(slots):
            c = col_2[0, k, tile]
            p = c // (2 * span) * span + lax.rem(c, span)
            g = p // (2 * tiles) * tiles + lax.rem(p, tiles)
            hots = columns(col_2, m2v, pairs2, tile, k, tiles, g)
            sub_copy(i, k).wait_recv()
            fin_a[i, k] = merged([lev_a[0, i, k]], [lev_a[1, i, k]], rows, [hots])[0]

    feat_near.wait()
    for i in range(quarter):
        tile = 4 * i + 2 * b + s
        rows = turned(m2v[pl.ds(first_group + tile, 1), :], width)
        at = pl.ds(i * width, width)
        total = lev_f[0, :, at].astype(jnp.float32) + right_side(lev_f[1, :, at], rows)
        fin_f[:, at] = total.astype(jnp.bfloat16)

    @pl.loop(0, quarter)
    def _(i):
        for q in range(groups):
            core_copy(0, i, q).wait_send()
            core_copy(1, i, q).wait_send()
        for k in range(slots):
            sub_copy(i, k).wait_send()


def put(tiles, feats, out_a, out_f, sem):
    copies = [
        pltpu.make_async_copy(tiles, out_a, sem.at[0]),
        pltpu.make_async_copy(feats, out_f, sem.at[1]),
    ]
    for copy in copies:
        copy.start()
    for copy in copies:
        copy.wait()


def per_device(features, adjacency, col_tiles, match_one, match_two):
    tiles, slots, width = adjacency.shape[:3]
    feats = features.shape[0]
    quarter, groups = tiles // 4, slots // GROUP
    span = lax.axis_size("sub") * tiles
    half = jnp.bfloat16

    def outside(part):
        return pltpu.with_memory_space_constraint(part, pltpu.HBM)

    dma = pltpu.SemaphoreType.DMA
    anywhere = pl.BlockSpec(memory_space=pltpu.HBM)
    inside = pl.BlockSpec(memory_space=pltpu.VMEM)
    tile_out = ((quarter, slots, width, width), half)
    feat_out = ((feats, quarter * width), half)
    done = pl.pallas_call(
        functools.partial(kernel, span),
        out_shape=(pltpu.VMEM(*tile_out), pltpu.VMEM(*feat_out)),
        in_specs=[anywhere] * 5,
        out_specs=(inside, inside),
        scratch_shapes=[
            pltpu.VMEM((match_one.shape[0] + 8, width), jnp.int32),
            pltpu.VMEM((match_two.shape[0] + 8, width), jnp.int32),
            pltpu.SMEM((2, slots, tiles), jnp.int32),
            pltpu.SMEM((2, slots, tiles), jnp.int32),
            pltpu.VMEM((2, 2, quarter, slots, width, width), half),
            pltpu.VMEM((2,) + features.shape, half),
            pltpu.VMEM((quarter, slots, width, width), half),
            pltpu.VMEM((feats, quarter * width), half),
            pltpu.VMEM((2, quarter, slots, width, width), half),
            pltpu.VMEM((2, feats, quarter * width), half),
            dma((5,)),
            dma((2, quarter, groups)),
            dma((2, quarter, groups)),
            dma((2, quarter, groups)),
            dma((quarter, slots)),
            dma((quarter, slots)),
            dma((4,)),
            dma((4,)),
        ],
        compiler_params=pltpu.CompilerParams(
            collective_id=0, has_side_effects=True, vmem_limit_bytes=VMEM_BYTES
        ),
        name="coarsen",
    )(*(outside(part) for part in (features, adjacency, col_tiles.T, match_one, match_two)))
    return pl.pallas_call(
        put,
        out_shape=(jax.ShapeDtypeStruct(*tile_out), jax.ShapeDtypeStruct(*feat_out)),
        in_specs=[inside] * 2,
        out_specs=(anywhere, anywhere),
        scratch_shapes=[dma((2,))],
        name="put",
    )(*(pltpu.with_memory_space_constraint(part, pltpu.VMEM) for part in done))


def solution(mesh):
    placed = (
        P(None, ("blk", "sub")),
        P(("blk", "sub"), None, None, None),
        P(("blk", "sub"), None),
        P(),
        P(),
    )
    return jax.shard_map(
        per_device,
        mesh=mesh,
        in_specs=placed,
        out_specs=(P(("blk", "sub"), None, None, None), P(None, ("blk", "sub"))),
        check_vma=False,
    )
```

time: 42.5 us -> 37.7 us (0.89)
  local copies, waits for them, and re-layouts: 4.99 us -> 0 us
    unnamed x3 -> x0, local copies, waits for them, and re-layouts: 4.99 us -> none
    pallas_call x1 -> x2, Pallas kernels: 36.6 us -> 37 us  [the longest x1 36 us: per_device(): pl.pallas_call(functools.partial(kernel, span), out_shape=(pltpu.VMEM(*ti...]
where the time goes in v2:
time: 37.7 us; the launch traced here: 37.6 us
  Pallas kernels  37 us (98%)
  between operations  0.64 us (2%)
    pallas_call x1, Pallas kernels, per_device(): pl.pallas_call(functools.partial(kernel, span), out_shape=(pltpu.VMEM(*ti...  36 us
    pallas_call x1, Pallas kernels, per_device(): pl.pallas_call(put, out_shape=(jax.ShapeDtypeStruct(*tile_out), jax.Shape...  0.99 us

profile of v2, /device:TPU:1, one launch (start us, length us, event | category | flops | bytes accessed | tf_op | source)
XLA Modules:
  0.0 37.6 jit_solution(7618467604445305351)
XLA Ops:
  0.6 36.0 %coarsen.1 = (bf16[4,8,128,128]{3,2,1,0:T(8,128)(2,1)S(1)}, bf16[16,512]{1,0:T(8,128)(2,1)S(1)}) custom-call(bf16[16,2048]{1,0:T(8,128)(2,1)} %feat.1, bf16[16,8,128,128]{3,2,1,0:T(8,128)(2,1)} %adj.1, s32[8,16]{1,0:T(8,128)} %bitcast.1, s32[4096,128]{1,0:T(8,128)} %m1.1, s32[2048,128]{1,0:T(8,128)} %m2.1), custom_call_target="tpu_custom_call" | custom-call | tf_op jit(solution)/shard_map/coarsen/pallas_call | solution.py:254
  36.6 1.0 %put.1 = (bf16[4,8,128,128]{3,2,1,0:T(8,128)(2,1)}, bf16[16,512]{1,0:T(8,128)(2,1)}) custom-call(bf16[4,8,128,128]{3,2,1,0:T(8,128)(2,1)S(1)} %get-tuple-element.4.tiles, bf16[16,512]{1,0:T(8,128)(2,1)S(1)} %get-tuple-element.5.feats), custom_call_target="tpu_custom_call" | custom-call | tf_op jit(solution)/shard_map/put/pallas_call | solution.py:284

commit v3 on v2

--- a/solution.py
+++ b/solution.py
@@ -9,6 +9,7 @@
 
 MESH = pl.DeviceIdType.MESH
 GROUP = 2
+LAST = (0, 0, 0, 0, 1, 1, 2, 3)
 VMEM_BYTES = 24 * 2**20
 
 
@@ -38,7 +39,7 @@
 def kernel(
     span, feat, adj, cols, m1, m2, fin_a, fin_f,
     m1v, m2v, col_1, col_2, adj_v, feat_v, send_a, send_f, lev_a, lev_f,
-    loc_sem, own_sem, cs_sem, cr_sem, ss_sem, sr_sem, xs_sem, xr_sem,
+    loc_sem, own_sem, cr_sem, sr_sem, send_sem, xr_sem,
 ):
     tiles, slots, width = adj.shape[0], adj.shape[1], adj.shape[2]
     quarter = tiles // 4
@@ -55,33 +56,34 @@
     def side(j):
         return (1 - s) * (1 - j) + s * j
 
-    def own_copy(j, i, q):
-        part = pl.ds(q * GROUP, GROUP)
+    def own_copy(j, i, part, n):
         return pltpu.make_async_copy(
-            adj.at[4 * i + 2 * b + side(j), part], adj_v.at[b, j, i, part], own_sem.at[j, i, q]
+            adj.at[4 * i + 2 * b + side(j), part], adj_v.at[b, j, i, part], own_sem.at[n]
         )
 
-    def core_copy(j, i, q):
-        part = pl.ds(q * GROUP, GROUP)
+    def core_copy(j, i, part, n):
         return pltpu.make_async_remote_copy(
             src_ref=adj.at[4 * i + 2 * (1 - b) + side(j), part],
             dst_ref=adj_v.at[b, j, i, part],
-            send_sem=cs_sem.at[j, i, q], recv_sem=cr_sem.at[j, i, q],
+            send_sem=send_sem.at[0], recv_sem=cr_sem.at[n],
             device_id=core, device_id_type=MESH,
         )
 
-    def sub_copy(i, k):
+    def sub_copy(i, k, n):
         return pltpu.make_async_remote_copy(
             src_ref=send_a.at[i, k], dst_ref=lev_a.at[s, i, k],
-            send_sem=ss_sem.at[i, k], recv_sem=sr_sem.at[i, k],
+            send_sem=send_sem.at[1], recv_sem=sr_sem.at[n],
             device_id=near, device_id_type=MESH,
         )
 
     def small(src, dst, n, device):
         return pltpu.make_async_remote_copy(
-            src_ref=src, dst_ref=dst, send_sem=xs_sem.at[n], recv_sem=xr_sem.at[n],
+            src_ref=src, dst_ref=dst, send_sem=send_sem.at[2 + n], recv_sem=xr_sem.at[n],
             device_id=device, device_id_type=MESH,
         )
+
+    def all_of(ref, sem):
+        pltpu.make_async_copy(ref, ref, sem).wait()
 
     barrier = pltpu.get_barrier_semaphore()
     pl.semaphore_signal(barrier, inc=1, device_id=core, device_id_type=MESH)
@@ -96,8 +98,11 @@
     ]
     for n in range(3):
         local[n].start()
+    whole = pl.ds(0, slots)
+    first = [pl.ds(q * GROUP, GROUP) for q in range(groups)]
+    last = quarter - 1
     for q in range(groups):
-        own_copy(0, 0, q).start()
+        own_copy(0, 0, first[q], q).start()
 
     plain = lax.broadcasted_iota(jnp.int32, (8, width), 1)
     m1v[pl.ds(pairs, 8), :] = plain
@@ -109,28 +114,26 @@
     feat_core = small(feat, feat_v.at[b], 2, core)
     cols_core.start()
     for q in range(groups):
-        core_copy(0, 0, q).start()
+        core_copy(0, 0, first[q], q).start()
+    feat_core.start()
     cols_near.start()
-    feat_core.start()
     local[3].start()
 
     @pl.loop(1, quarter)
     def _(i):
-        for q in range(groups):
-            core_copy(0, i, q).start()
-            own_copy(0, i, q).start()
+        core_copy(0, i, whole, groups - 1 + i).start()
+        own_copy(0, i, whole, groups - 1 + i).start()
 
     @pl.loop(0, quarter)
     def _(i):
-        for q in range(groups):
-            core_copy(1, i, q).start()
-            own_copy(1, i, q).start()
+        core_copy(1, i, whole, groups - 1 + quarter + i).start()
+        own_copy(1, i, whole, groups - 1 + quarter + i).start()
 
     local[4].start()
 
     for n in range(3):
         local[n].wait()
-    cols_core.wait()
+    cols_core.wait_recv()
 
     def columns(table, maps, plain_row, tile, k, bit, row):
         hots = []
@@ -140,12 +143,16 @@
             hots.append(turned(here, width))
         return jnp.concatenate(hots, axis=1)
 
-    def first_level(j, i, store):
+    def first_rows(tile):
+        return turned(m1v[pl.ds(first_pair + tile, 1), :], width)
+
+    def first_level(j, i, store, parts):
         tile = 4 * i + 2 * b + side(j)
-        rows = turned(m1v[pl.ds(first_pair + tile, 1), :], width)
+        rows = first_rows(tile)
         for q in range(groups):
-            own_copy(j, i, q).wait()
-            core_copy(j, i, q).wait_recv()
+            for part, n in parts.get(q, ()):
+                own_copy(j, i, part, n).wait()
+                core_copy(j, i, part, n).wait_recv()
             ks = range(q * GROUP, (q + 1) * GROUP)
             hots = []
             for k in ks:
@@ -155,7 +162,7 @@
             done = merged(
                 [adj_v[0, j, i, k] for k in ks], [adj_v[1, j, i, k] for k in ks], rows, hots
             )
-            store(i, q, ks, done)
+            store(i, ks, done)
         return tile, rows
 
     def feature_level(j, i, tile, rows, dst):
@@ -163,66 +170,80 @@
         total = feat_v[0, :, at].astype(jnp.float32) + right_side(feat_v[1, :, at], rows)
         dst[:, pl.ds(pl.multiple_of(i * width, width), width)] = total.astype(jnp.bfloat16)
 
-    def store_send(i, q, ks, done):
-        for k, block in zip(ks, done):
-            send_a[i, k] = block
-            sub_copy(i, k).start()
-
-    def store_keep(i, q, ks, done):
+    def store_send(arrival):
+        def store(i, ks, done):
+            for k, block in zip(ks, done):
+                send_a[i, k] = block
+                sub_copy(i, k, arrival(i, k)).start()
+
+        return store
+
+    def store_keep(i, ks, done):
         for k, block in zip(ks, done):
             lev_a[s, i, k] = block
 
-    @pl.loop(0, quarter)
-    def _(i):
-        first_level(0, i, store_send)
+    def last_arrival(i, k):
+        return last + LAST[k]
+
+    first_level(0, 0, store_send(lambda i, k: 0), {q: [(first[q], q)] for q in range(groups)})
 
     local[3].wait()
-    feat_core.wait()
-
-    @pl.loop(0, quarter)
-    def _(i):
+    feat_core.wait_recv()
+    for i in range(quarter):
         tile = 4 * i + 2 * b + side(0)
-        rows = turned(m1v[pl.ds(first_pair + tile, 1), :], width)
-        feature_level(0, i, tile, rows, send_f)
-
+        feature_level(0, i, tile, first_rows(tile), send_f)
     feat_near = small(send_f, lev_f.at[s], 3, near)
     feat_near.start()
 
+    @pl.loop(1, last)
+    def _(i):
+        first_level(0, i, store_send(lambda i, k: i), {0: [(whole, groups - 1 + i)]})
+
+    first_level(0, last, store_send(last_arrival), {0: [(whole, groups - 1 + last)]})
+
     @pl.loop(0, quarter)
     def _(i):
-        tile, rows = first_level(1, i, store_keep)
+        tile, rows = first_level(1, i, store_keep, {0: [(whole, groups - 1 + quarter + i)]})
         feature_level(1, i, tile, rows, lev_f.at[s])
 
     local[4].wait()
-    cols_near.wait()
-
-    @pl.loop(0, quarter)
-    def _(i):
+    cols_near.wait_recv()
+
+    def second_rows(tile):
+        return turned(m2v[pl.ds(first_group + tile, 1), :], width)
+
+    def second_level(i, waits):
         tile = 4 * i + 2 * b + s
-        rows = turned(m2v[pl.ds(first_group + tile, 1), :], width)
+        rows = second_rows(tile)
         for k in range(slots):
             c = col_2[0, k, tile]
             p = c // (2 * span) * span + lax.rem(c, span)
             g = p // (2 * tiles) * tiles + lax.rem(p, tiles)
             hots = columns(col_2, m2v, pairs2, tile, k, tiles, g)
-            sub_copy(i, k).wait_recv()
+            if k in waits:
+                count, n = waits[k]
+                all_of(lev_a.at[1 - s, i, pl.ds(k, count)], sr_sem.at[n])
             fin_a[i, k] = merged([lev_a[0, i, k]], [lev_a[1, i, k]], rows, [hots])[0]
 
-    feat_near.wait()
+    @pl.loop(0, last)
+    def _(i):
+        second_level(i, {0: (slots, i)})
+
+    feat_near.wait_recv()
     for i in range(quarter):
-        tile = 4 * i + 2 * b + s
-        rows = turned(m2v[pl.ds(first_group + tile, 1), :], width)
         at = pl.ds(i * width, width)
+        rows = second_rows(4 * i + 2 * b + s)
         total = lev_f[0, :, at].astype(jnp.float32) + right_side(lev_f[1, :, at], rows)
         fin_f[:, at] = total.astype(jnp.bfloat16)
 
-    @pl.loop(0, quarter)
-    def _(i):
-        for q in range(groups):
-            core_copy(0, i, q).wait_send()
-            core_copy(1, i, q).wait_send()
-        for k in range(slots):
-            sub_copy(i, k).wait_send()
+    second_level(
+        last, {LAST.index(n): (LAST.count(n), last + n) for n in range(max(LAST) + 1)}
+    )
+
+    all_of(adj_v.at[0], send_sem.at[0])
+    all_of(send_a, send_sem.at[1])
+    for copy in (cols_core, cols_near, feat_core, feat_near):
+        copy.wait_send()
 
 
 def put(tiles, feats, out_a, out_f, sem):
@@ -268,12 +289,10 @@
             pltpu.VMEM((2, quarter, slots, width, width), half),
             pltpu.VMEM((2, feats, quarter * width), half),
             dma((5,)),
-            dma((2, quarter, groups)),
-            dma((2, quarter, groups)),
-            dma((2, quarter, groups)),
-            dma((quarter, slots)),
-            dma((quarter, slots)),
-            dma((4,)),
+            dma((groups - 1 + 2 * quarter,)),
+            dma((groups - 1 + 2 * quarter,)),
+            dma((quarter + max(LAST),)),
+            dma((6,)),
             dma((4,)),
         ],
         compiler_params=pltpu.CompilerParams(

time: 37.7 us -> 36.3 us (0.963)
  Pallas kernels: 37 us -> 35.5 us
    pallas_call x1, Pallas kernels: 36 us -> 34.5 us  [per_device(): pl.pallas_call(functools.partial(kernel, span), out_shape=(pltpu.VMEM(*ti...]
where the time goes in v3:
time: 36.3 us; the launch traced here: 36.2 us
  Pallas kernels  35.5 us (98%)
  between operations  0.64 us (2%)
    pallas_call x1, Pallas kernels, per_device(): pl.pallas_call(functools.partial(kernel, span), out_shape=(pltpu.VMEM(*ti...  34.5 us
    pallas_call x1, Pallas kernels, per_device(): pl.pallas_call(put, out_shape=(jax.ShapeDtypeStruct(*tile_out), jax.Shape...  0.99 us

profile of v3, /device:TPU:1, one launch (start us, length us, event | category | flops | bytes accessed | tf_op | source)
XLA Modules:
  0.0 36.2 jit_solution(8481843319774684482)
XLA Ops:
  0.6 34.5 %coarsen.1 = (bf16[4,8,128,128]{3,2,1,0:T(8,128)(2,1)S(1)}, bf16[16,512]{1,0:T(8,128)(2,1)S(1)}) custom-call(bf16[16,2048]{1,0:T(8,128)(2,1)} %feat.1, bf16[16,8,128,128]{3,2,1,0:T(8,128)(2,1)} %adj.1, s32[8,16]{1,0:T(8,128)} %bitcast.1, s32[4096,128]{1,0:T(8,128)} %m1.1, s32[2048,128]{1,0:T(8,128)} %m2.1), custom_call_target="tpu_custom_call" | custom-call | tf_op jit(solution)/shard_map/coarsen/pallas_call | solution.py:275
  35.2 1.0 %put.1 = (bf16[4,8,128,128]{3,2,1,0:T(8,128)(2,1)}, bf16[16,512]{1,0:T(8,128)(2,1)}) custom-call(bf16[4,8,128,128]{3,2,1,0:T(8,128)(2,1)S(1)} %get-tuple-element.4.tiles, bf16[16,512]{1,0:T(8,128)(2,1)S(1)} %get-tuple-element.5.feats), custom_call_target="tpu_custom_call" | custom-call | tf_op jit(solution)/shard_map/put/pallas_call | solution.py:303

commit v4 on v3

--- a/solution.py
+++ b/solution.py
@@ -10,6 +10,8 @@
 MESH = pl.DeviceIdType.MESH
 GROUP = 2
 LAST = (0, 0, 0, 0, 1, 1, 2, 3)
+RAW = 1
+LAG = 2
 VMEM_BYTES = 24 * 2**20
 
 
@@ -38,8 +40,8 @@
 
 def kernel(
     span, feat, adj, cols, m1, m2, fin_a, fin_f,
-    m1v, m2v, col_1, col_2, adj_v, feat_v, send_a, send_f, lev_a, lev_f,
-    loc_sem, own_sem, cr_sem, sr_sem, send_sem, xr_sem,
+    m1v, m2v, col_1, col_2, col_3, raw_v, adj_v, feat_v, send_a, send_f, lev_a, lev_f,
+    loc_sem, got_sem, sr_sem, send_sem, xr_sem,
 ):
     tiles, slots, width = adj.shape[0], adj.shape[1], adj.shape[2]
     quarter = tiles // 4
@@ -48,6 +50,7 @@
     b, s = lax.rem(blk, 2), lax.rem(sub, 2)
     core = {"blk": blk + 1 - 2 * b}
     near = {"sub": sub + 1 - 2 * s}
+    across = {"blk": blk + 1 - 2 * b, "sub": sub + 1 - 2 * s}
     subs = span // tiles
     first_pair = (blk // 2 * subs + sub) * tiles
     first_group = (blk // 2 * (subs // 2) + sub // 2) * tiles
@@ -58,20 +61,20 @@
 
     def own_copy(j, i, part, n):
         return pltpu.make_async_copy(
-            adj.at[4 * i + 2 * b + side(j), part], adj_v.at[b, j, i, part], own_sem.at[n]
+            adj.at[4 * i + 2 * b + side(j), part], adj_v.at[b, j, i, part], got_sem.at[n]
         )
 
     def core_copy(j, i, part, n):
         return pltpu.make_async_remote_copy(
             src_ref=adj.at[4 * i + 2 * (1 - b) + side(j), part],
             dst_ref=adj_v.at[b, j, i, part],
-            send_sem=send_sem.at[0], recv_sem=cr_sem.at[n],
+            send_sem=send_sem.at[0], recv_sem=got_sem.at[n],
             device_id=core, device_id_type=MESH,
         )
 
     def sub_copy(i, k, n):
         return pltpu.make_async_remote_copy(
-            src_ref=send_a.at[i, k], dst_ref=lev_a.at[s, i, k],
+            src_ref=send_a.at[i * slots + k], dst_ref=lev_a.at[s, i, k],
             send_sem=send_sem.at[1], recv_sem=sr_sem.at[n],
             device_id=near, device_id_type=MESH,
         )
@@ -88,6 +91,7 @@
     barrier = pltpu.get_barrier_semaphore()
     pl.semaphore_signal(barrier, inc=1, device_id=core, device_id_type=MESH)
     pl.semaphore_signal(barrier, inc=1, device_id=near, device_id_type=MESH)
+    pl.semaphore_signal(barrier, inc=1, device_id=across, device_id_type=MESH)
 
     local = [
         pltpu.make_async_copy(m1, m1v.at[pl.ds(0, pairs)], loc_sem.at[0]),
@@ -99,24 +103,32 @@
     for n in range(3):
         local[n].start()
     whole = pl.ds(0, slots)
-    first = [pl.ds(q * GROUP, GROUP) for q in range(groups)]
+    first = [pl.ds(max(RAW, q * GROUP), (q + 1) * GROUP - max(RAW, q * GROUP)) for q in range(groups)]
+    late = [q for q in range(groups) if (q + 1) * GROUP > RAW]
     last = quarter - 1
-    for q in range(groups):
+    for q in late:
         own_copy(0, 0, first[q], q).start()
 
     plain = lax.broadcasted_iota(jnp.int32, (8, width), 1)
     m1v[pl.ds(pairs, 8), :] = plain
     m2v[pl.ds(pairs2, 8), :] = plain
 
-    pl.semaphore_wait(barrier, 2)
+    pl.semaphore_wait(barrier, 3)
     cols_core = small(cols, col_1.at[b], 0, core)
     cols_near = small(cols, col_2.at[s], 1, near)
     feat_core = small(feat, feat_v.at[b], 2, core)
     cols_core.start()
-    for q in range(groups):
+    for q in late:
         core_copy(0, 0, first[q], q).start()
+    early = pl.ds(0, RAW)
+    raw_near = small(adj.at[2 * b + side(0), early], raw_v.at[b], 4, near)
+    raw_across = small(adj.at[2 * (1 - b) + side(0), early], raw_v.at[b], 5, across)
+    raw_near.start()
+    raw_across.start()
+    cols_across = small(cols, col_3, 6, across)
     feat_core.start()
     cols_near.start()
+    cols_across.start()
     local[3].start()
 
     @pl.loop(1, quarter)
@@ -146,14 +158,15 @@
     def first_rows(tile):
         return turned(m1v[pl.ds(first_pair + tile, 1), :], width)
 
-    def first_level(j, i, store, parts):
+    def first_level(j, i, store, parts, start=0):
         tile = 4 * i + 2 * b + side(j)
         rows = first_rows(tile)
         for q in range(groups):
             for part, n in parts.get(q, ()):
-                own_copy(j, i, part, n).wait()
-                core_copy(j, i, part, n).wait_recv()
-            ks = range(q * GROUP, (q + 1) * GROUP)
+                all_of(adj_v.at[:, j, i, part], got_sem.at[n])
+            ks = range(max(start, q * GROUP), (q + 1) * GROUP)
+            if not ks:
+                continue
             hots = []
             for k in ks:
                 c = col_1[0, k, tile]
@@ -170,22 +183,30 @@
         total = feat_v[0, :, at].astype(jnp.float32) + right_side(feat_v[1, :, at], rows)
         dst[:, pl.ds(pl.multiple_of(i * width, width), width)] = total.astype(jnp.bfloat16)
 
-    def store_send(arrival):
-        def store(i, ks, done):
-            for k, block in zip(ks, done):
-                send_a[i, k] = block
+    def arrival(i, k):
+        return last + LAST[k] if isinstance(i, int) and i == last else i
+
+    def store_send(i, ks, done):
+        for k, block in zip(ks, done):
+            send_a[i * slots + k] = block
+
+        @pl.when(b == 1)
+        def _():
+            for k in ks:
                 sub_copy(i, k, arrival(i, k)).start()
 
-        return store
+    def send_tile(i, begin):
+        @pl.when(b == 0)
+        def _():
+            for k in range(begin, slots):
+                sub_copy(i, k, arrival(i, k)).start()
+
 
     def store_keep(i, ks, done):
         for k, block in zip(ks, done):
             lev_a[s, i, k] = block
 
-    def last_arrival(i, k):
-        return last + LAST[k]
-
-    first_level(0, 0, store_send(lambda i, k: 0), {q: [(first[q], q)] for q in range(groups)})
+    first_level(0, 0, store_send, {q: [(first[q], q)] for q in late}, RAW)
 
     local[3].wait()
     feat_core.wait_recv()
@@ -195,11 +216,12 @@
     feat_near = small(send_f, lev_f.at[s], 3, near)
     feat_near.start()
 
-    @pl.loop(1, last)
-    def _(i):
-        first_level(0, i, store_send(lambda i, k: i), {0: [(whole, groups - 1 + i)]})
-
-    first_level(0, last, store_send(last_arrival), {0: [(whole, groups - 1 + last)]})
+    for i in range(1, quarter):
+        first_level(0, i, store_send, {0: [(whole, groups - 1 + i)]})
+        if i >= LAG:
+            send_tile(i - LAG, RAW if i == LAG else 0)
+    for i in range(quarter - LAG, quarter):
+        send_tile(i, RAW if i == 0 else 0)
 
     @pl.loop(0, quarter)
     def _(i):
@@ -207,7 +229,27 @@
         feature_level(1, i, tile, rows, lev_f.at[s])
 
     local[4].wait()
-    cols_near.wait_recv()
+    for copy in (cols_near, cols_across, raw_near, raw_across):
+        copy.wait_recv()
+    there = 2 * b + s
+    near_pair = (blk // 2 * subs + sub + 1 - 2 * s) * tiles
+    near_rows = turned(m1v[pl.ds(near_pair + there, 1), :], width)
+    hots = []
+    for k in range(RAW):
+        c = col_2[1 - s, k, there]
+        p = c // (2 * span) * span + lax.rem(c, span)
+        mine = lax.rem(c // span, 2)
+        other = lax.rem(col_3[k, there] // span, 2)
+        parts = []
+        for upper in (b * other + (1 - b) * mine, b * mine + (1 - b) * other):
+            row = upper * p + (1 - upper) * pairs
+            parts.append(turned(m1v[pl.ds(row, 1), :], width))
+        hots.append(jnp.concatenate(parts, axis=1))
+    done = merged(
+        [raw_v[0, k] for k in range(RAW)], [raw_v[1, k] for k in range(RAW)], near_rows, hots
+    )
+    for k in range(RAW):
+        lev_a[1 - s, 0, k] = done[k]
 
     def second_rows(tile):
         return turned(m2v[pl.ds(first_group + tile, 1), :], width)
@@ -225,7 +267,9 @@
                 all_of(lev_a.at[1 - s, i, pl.ds(k, count)], sr_sem.at[n])
             fin_a[i, k] = merged([lev_a[0, i, k]], [lev_a[1, i, k]], rows, [hots])[0]
 
-    @pl.loop(0, last)
+    second_level(0, {RAW: (slots - RAW, 0)})
+
+    @pl.loop(1, last)
     def _(i):
         second_level(i, {0: (slots, i)})
 
@@ -240,9 +284,11 @@
         last, {LAST.index(n): (LAST.count(n), last + n) for n in range(max(LAST) + 1)}
     )
 
-    all_of(adj_v.at[0], send_sem.at[0])
-    all_of(send_a, send_sem.at[1])
-    for copy in (cols_core, cols_near, feat_core, feat_near):
+    all_of(adj_v.at[0, 0, 0, pl.ds(RAW, slots - RAW)], send_sem.at[0])
+    all_of(adj_v.at[0, 0, pl.ds(1, last)], send_sem.at[0])
+    all_of(adj_v.at[0, 1], send_sem.at[0])
+    all_of(send_a.at[pl.ds(RAW, quarter * slots - RAW)], send_sem.at[1])
+    for copy in (cols_core, cols_near, cols_across, feat_core, feat_near, raw_near, raw_across):
         copy.wait_send()
 
 
@@ -282,18 +328,19 @@
             pltpu.VMEM((match_two.shape[0] + 8, width), jnp.int32),
             pltpu.SMEM((2, slots, tiles), jnp.int32),
             pltpu.SMEM((2, slots, tiles), jnp.int32),
+            pltpu.SMEM((slots, tiles), jnp.int32),
+            pltpu.VMEM((2, RAW, width, width), half),
             pltpu.VMEM((2, 2, quarter, slots, width, width), half),
             pltpu.VMEM((2,) + features.shape, half),
-            pltpu.VMEM((quarter, slots, width, width), half),
+            pltpu.VMEM((quarter * slots, width, width), half),
             pltpu.VMEM((feats, quarter * width), half),
             pltpu.VMEM((2, quarter, slots, width, width), half),
             pltpu.VMEM((2, feats, quarter * width), half),
             dma((5,)),
             dma((groups - 1 + 2 * quarter,)),
-            dma((groups - 1 + 2 * quarter,)),
             dma((quarter + max(LAST),)),
-            dma((6,)),
-            dma((4,)),
+            dma((9,)),
+            dma((7,)),
         ],
         compiler_params=pltpu.CompilerParams(
             collective_id=0, has_side_effects=True, vmem_limit_bytes=VMEM_BYTES

time: 36.3 us -> 34.2 us (0.942)
  the two profiles are of different devices: /device:TPU:1 before, /device:TPU:8 now
where the time goes in v4:
time: 34.2 us; the launch traced here: 34.1 us
  Pallas kernels  33.5 us (98%)
  between operations  0.64 us (2%)
    pallas_call x1, Pallas kernels, per_device(): pl.pallas_call(functools.partial(kernel, span), out_shape=(pltpu.VMEM(*ti...  32.5 us
    pallas_call x1, Pallas kernels, per_device(): pl.pallas_call(put, out_shape=(jax.ShapeDtypeStruct(*tile_out), jax.Shape...  0.99 us

profile of v4, /device:TPU:8, one launch (start us, length us, event | category | flops | bytes accessed | tf_op | source)
XLA Modules:
  0.0 34.1 jit_solution(12249798244683822657)
XLA Ops:
  0.6 32.5 %coarsen.1 = (bf16[4,8,128,128]{3,2,1,0:T(8,128)(2,1)S(1)}, bf16[16,512]{1,0:T(8,128)(2,1)S(1)}) custom-call(bf16[16,2048]{1,0:T(8,128)(2,1)} %feat.1, bf16[16,8,128,128]{3,2,1,0:T(8,128)(2,1)} %adj.1, s32[8,16]{1,0:T(8,128)} %bitcast.1, s32[4096,128]{1,0:T(8,128)} %m1.1, s32[2048,128]{1,0:T(8,128)} %m2.1), custom_call_target="tpu_custom_call" | custom-call | tf_op jit(solution)/shard_map/coarsen/pallas_call | solution.py:321
  33.1 1.0 %put.1 = (bf16[4,8,128,128]{3,2,1,0:T(8,128)(2,1)}, bf16[16,512]{1,0:T(8,128)(2,1)}) custom-call(bf16[4,8,128,128]{3,2,1,0:T(8,128)(2,1)S(1)} %get-tuple-element.4.tiles, bf16[16,512]{1,0:T(8,128)(2,1)S(1)} %get-tuple-element.5.feats), custom_call_target="tpu_custom_call" | custom-call | tf_op jit(solution)/shard_map/put/pallas_call | solution.py:350

commit v5 on v4

--- a/solution.py
+++ b/solution.py
@@ -9,7 +9,7 @@
 
 MESH = pl.DeviceIdType.MESH
 GROUP = 2
-LAST = (0, 0, 0, 0, 1, 1, 2, 3)
+LAST = (0, 0, 0, 0, 0, 0, 1, 2)
 RAW = 1
 LAG = 2
 VMEM_BYTES = 24 * 2**20
@@ -36,6 +36,17 @@
         both = jnp.concatenate([block, moved[:, n * width : (n + 1) * width]], axis=1)
         out.append(right_side(both, turned_cols[n]).astype(jnp.bfloat16))
     return out
+
+
+def carried(blocks, turned_rows, turned_cols):
+    width = turned_rows.shape[0]
+    moved = jnp.dot(
+        turned_rows, jnp.concatenate(blocks, axis=1), preferred_element_type=jnp.float32
+    ).astype(jnp.bfloat16)
+    return [
+        right_side(moved[:, n * width : (n + 1) * width], turned_cols[n]).astype(jnp.bfloat16)
+        for n in range(len(blocks))
+    ]
 
 
 def kernel(
@@ -68,20 +79,20 @@
         return pltpu.make_async_remote_copy(
             src_ref=adj.at[4 * i + 2 * (1 - b) + side(j), part],
             dst_ref=adj_v.at[b, j, i, part],
-            send_sem=send_sem.at[0], recv_sem=got_sem.at[n],
+            send_sem=send_sem, recv_sem=got_sem.at[n],
             device_id=core, device_id_type=MESH,
         )
 
     def sub_copy(i, k, n):
         return pltpu.make_async_remote_copy(
             src_ref=send_a.at[i * slots + k], dst_ref=lev_a.at[s, i, k],
-            send_sem=send_sem.at[1], recv_sem=sr_sem.at[n],
+            send_sem=send_sem, recv_sem=sr_sem.at[n],
             device_id=near, device_id_type=MESH,
         )
 
     def small(src, dst, n, device):
         return pltpu.make_async_remote_copy(
-            src_ref=src, dst_ref=dst, send_sem=send_sem.at[2 + n], recv_sem=xr_sem.at[n],
+            src_ref=src, dst_ref=dst, send_sem=send_sem, recv_sem=xr_sem.at[n],
             device_id=device, device_id_type=MESH,
         )
 
@@ -103,10 +114,11 @@
     for n in range(3):
         local[n].start()
     whole = pl.ds(0, slots)
-    first = [pl.ds(max(RAW, q * GROUP), (q + 1) * GROUP - max(RAW, q * GROUP)) for q in range(groups)]
-    late = [q for q in range(groups) if (q + 1) * GROUP > RAW]
+    edges = (RAW, GROUP, 2 * GROUP, slots)
+    first = [pl.ds(low, high - low) for low, high in zip(edges, edges[1:])]
+    heads = len(first) - 1
     last = quarter - 1
-    for q in late:
+    for q in range(heads + 1):
         own_copy(0, 0, first[q], q).start()
 
     plain = lax.broadcasted_iota(jnp.int32, (8, width), 1)
@@ -118,7 +130,7 @@
     cols_near = small(cols, col_2.at[s], 1, near)
     feat_core = small(feat, feat_v.at[b], 2, core)
     cols_core.start()
-    for q in late:
+    for q in range(heads + 1):
         core_copy(0, 0, first[q], q).start()
     early = pl.ds(0, RAW)
     raw_near = small(adj.at[2 * b + side(0), early], raw_v.at[b], 4, near)
@@ -131,17 +143,9 @@
     cols_across.start()
     local[3].start()
 
-    @pl.loop(1, quarter)
-    def _(i):
-        core_copy(0, i, whole, groups - 1 + i).start()
-        own_copy(0, i, whole, groups - 1 + i).start()
-
-    @pl.loop(0, quarter)
-    def _(i):
-        core_copy(1, i, whole, groups - 1 + quarter + i).start()
-        own_copy(1, i, whole, groups - 1 + quarter + i).start()
-
-    local[4].start()
+    core_copy(0, 1, whole, heads + 1).start()
+    own_copy(0, 1, whole, heads + 1).start()
+
 
     for n in range(3):
         local[n].wait()
@@ -186,7 +190,22 @@
     def arrival(i, k):
         return last + LAST[k] if isinstance(i, int) and i == last else i
 
+    def own_second(j, ks, done):
+        tile = 4 * last + 2 * b + side(j)
+        high = s * (first_group + tile) + (1 - s) * pairs2
+        rows = turned(m2v[pl.ds(high, 1), :], width)
+        hots = []
+        for k in ks:
+            c = col_2[s, k, tile]
+            p = c // (2 * span) * span + lax.rem(c, span)
+            g = p // (2 * tiles) * tiles + lax.rem(p, tiles)
+            upper = lax.rem(c // tiles, 2)
+            hots.append(turned(m2v[pl.ds(upper * g + (1 - upper) * pairs2, 1), :], width))
+        return carried(done, rows, hots)
+
     def store_send(i, ks, done):
+        if i == last:
+            done = own_second(0, ks, done)
         for k, block in zip(ks, done):
             send_a[i * slots + k] = block
 
@@ -203,11 +222,24 @@
 
 
     def store_keep(i, ks, done):
+        if isinstance(i, int):
+            done = own_second(1, ks, done)
         for k, block in zip(ks, done):
             lev_a[s, i, k] = block
 
-    first_level(0, 0, store_send, {q: [(first[q], q)] for q in late}, RAW)
-
+    first_level(0, 0, store_send, {q: [(first[q], q)] for q in range(heads + 1)}, RAW)
+
+    @pl.loop(2, quarter)
+    def _(i):
+        core_copy(0, i, whole, heads + i).start()
+        own_copy(0, i, whole, heads + i).start()
+
+    @pl.loop(0, quarter)
+    def _(i):
+        core_copy(1, i, whole, heads + quarter + i).start()
+        own_copy(1, i, whole, heads + quarter + i).start()
+
+    local[4].start()
     local[3].wait()
     feat_core.wait_recv()
     for i in range(quarter):
@@ -217,18 +249,21 @@
     feat_near.start()
 
     for i in range(1, quarter):
-        first_level(0, i, store_send, {0: [(whole, groups - 1 + i)]})
+        if i == last:
+            local[4].wait()
+        first_level(0, i, store_send, {0: [(whole, heads + i)]})
         if i >= LAG:
             send_tile(i - LAG, RAW if i == LAG else 0)
     for i in range(quarter - LAG, quarter):
         send_tile(i, RAW if i == 0 else 0)
 
-    @pl.loop(0, quarter)
-    def _(i):
-        tile, rows = first_level(1, i, store_keep, {0: [(whole, groups - 1 + quarter + i)]})
+    def keep(i):
+        tile, rows = first_level(1, i, store_keep, {0: [(whole, heads + quarter + i)]})
         feature_level(1, i, tile, rows, lev_f.at[s])
 
-    local[4].wait()
+    pl.loop(0, last)(keep)
+    keep(last)
+
     for copy in (cols_near, cols_across, raw_near, raw_across):
         copy.wait_recv()
     there = 2 * b + s
@@ -254,7 +289,7 @@
     def second_rows(tile):
         return turned(m2v[pl.ds(first_group + tile, 1), :], width)
 
-    def second_level(i, waits):
+    def second_level(i, begin):
         tile = 4 * i + 2 * b + s
         rows = second_rows(tile)
         for k in range(slots):
@@ -262,16 +297,15 @@
             p = c // (2 * span) * span + lax.rem(c, span)
             g = p // (2 * tiles) * tiles + lax.rem(p, tiles)
             hots = columns(col_2, m2v, pairs2, tile, k, tiles, g)
-            if k in waits:
-                count, n = waits[k]
-                all_of(lev_a.at[1 - s, i, pl.ds(k, count)], sr_sem.at[n])
+            if k == begin:
+                all_of(lev_a.at[1 - s, i, pl.ds(k, slots - k)], sr_sem.at[i])
             fin_a[i, k] = merged([lev_a[0, i, k]], [lev_a[1, i, k]], rows, [hots])[0]
 
-    second_level(0, {RAW: (slots - RAW, 0)})
+    second_level(0, RAW)
 
     @pl.loop(1, last)
     def _(i):
-        second_level(i, {0: (slots, i)})
+        second_level(i, 0)
 
     feat_near.wait_recv()
     for i in range(quarter):
@@ -280,14 +314,16 @@
         total = lev_f[0, :, at].astype(jnp.float32) + right_side(lev_f[1, :, at], rows)
         fin_f[:, at] = total.astype(jnp.bfloat16)
 
-    second_level(
-        last, {LAST.index(n): (LAST.count(n), last + n) for n in range(max(LAST) + 1)}
-    )
-
-    all_of(adj_v.at[0, 0, 0, pl.ds(RAW, slots - RAW)], send_sem.at[0])
-    all_of(adj_v.at[0, 0, pl.ds(1, last)], send_sem.at[0])
-    all_of(adj_v.at[0, 1], send_sem.at[0])
-    all_of(send_a.at[pl.ds(RAW, quarter * slots - RAW)], send_sem.at[1])
+    for n in range(max(LAST) + 1):
+        part = pl.ds(LAST.index(n), LAST.count(n))
+        all_of(lev_a.at[1 - s, last, part], sr_sem.at[last + n])
+        total = lev_a[0, last, part].astype(jnp.float32) + lev_a[1, last, part].astype(jnp.float32)
+        fin_a[last, part] = total.astype(jnp.bfloat16)
+
+    all_of(adj_v.at[0, 0, 0, pl.ds(RAW, slots - RAW)], send_sem)
+    all_of(adj_v.at[0, 0, pl.ds(1, last)], send_sem)
+    all_of(adj_v.at[0, 1], send_sem)
+    all_of(send_a.at[pl.ds(RAW, quarter * slots - RAW)], send_sem)
     for copy in (cols_core, cols_near, cols_across, feat_core, feat_near, raw_near, raw_across):
         copy.wait_send()
 
@@ -337,9 +373,9 @@
             pltpu.VMEM((2, quarter, slots, width, width), half),
             pltpu.VMEM((2, feats, quarter * width), half),
             dma((5,)),
-            dma((groups - 1 + 2 * quarter,)),
+            dma((2 + 2 * quarter,)),
             dma((quarter + max(LAST),)),
-            dma((9,)),
+            dma,
             dma((7,)),
         ],
         compiler_params=pltpu.CompilerParams(

time: 34.2 us -> 33.9 us (level)
  Pallas kernels: 33.5 us -> 33.1 us
    pallas_call x1, Pallas kernels: 32.5 us -> 32.1 us  [per_device(): pl.pallas_call(functools.partial(kernel, span), out_shape=(pltpu.VMEM(*ti...]
where the time goes in v5:
time: 33.9 us; the launch traced here: 33.7 us
  Pallas kernels  33.1 us (98%)
  between operations  0.64 us (2%)
    pallas_call x1, Pallas kernels, per_device(): pl.pallas_call(functools.partial(kernel, span), out_shape=(pltpu.VMEM(*ti...  32.1 us
    pallas_call x1, Pallas kernels, per_device(): pl.pallas_call(put, out_shape=(jax.ShapeDtypeStruct(*tile_out), jax.Shape...  0.99 us

profile of v5, /device:TPU:8, one launch (start us, length us, event | category | flops | bytes accessed | tf_op | source)
XLA Modules:
  0.0 33.7 jit_solution(14768595938045269090)
XLA Ops:
  0.6 32.1 %coarsen.1 = (bf16[4,8,128,128]{3,2,1,0:T(8,128)(2,1)S(1)}, bf16[16,512]{1,0:T(8,128)(2,1)S(1)}) custom-call(bf16[16,2048]{1,0:T(8,128)(2,1)} %feat.1, bf16[16,8,128,128]{3,2,1,0:T(8,128)(2,1)} %adj.1, s32[8,16]{1,0:T(8,128)} %bitcast.1, s32[4096,128]{1,0:T(8,128)} %m1.1, s32[2048,128]{1,0:T(8,128)} %m2.1), custom_call_target="tpu_custom_call" | custom-call | tf_op jit(solution)/shard_map/coarsen/pallas_call | solution.py:357
  32.7 1.0 %put.1 = (bf16[4,8,128,128]{3,2,1,0:T(8,128)(2,1)}, bf16[16,512]{1,0:T(8,128)(2,1)}) custom-call(bf16[4,8,128,128]{3,2,1,0:T(8,128)(2,1)S(1)} %get-tuple-element.4.tiles, bf16[16,512]{1,0:T(8,128)(2,1)S(1)} %get-tuple-element.5.feats), custom_call_target="tpu_custom_call" | custom-call | tf_op jit(solution)/shard_map/put/pallas_call | solution.py:386

commit v6 on v5

--- a/solution.py
+++ b/solution.py
@@ -51,7 +51,7 @@
 
 def kernel(
     span, feat, adj, cols, m1, m2, fin_a, fin_f,
-    m1v, m2v, col_1, col_2, col_3, raw_v, adj_v, feat_v, send_a, send_f, lev_a, lev_f,
+    m1v, m2v, tab, raw_v, adj_v, feat_v, send_a, send_f, lev_a, lev_f,
     loc_sem, got_sem, sr_sem, send_sem, xr_sem,
 ):
     tiles, slots, width = adj.shape[0], adj.shape[1], adj.shape[2]
@@ -106,55 +106,54 @@
 
     local = [
         pltpu.make_async_copy(m1, m1v.at[pl.ds(0, pairs)], loc_sem.at[0]),
-        pltpu.make_async_copy(cols, col_1.at[b], loc_sem.at[1]),
-        pltpu.make_async_copy(cols, col_2.at[s], loc_sem.at[2]),
-        pltpu.make_async_copy(feat, feat_v.at[b], loc_sem.at[3]),
-        pltpu.make_async_copy(m2, m2v.at[pl.ds(0, pairs2)], loc_sem.at[4]),
+        pltpu.make_async_copy(cols, tab.at[b], loc_sem.at[1]),
+        pltpu.make_async_copy(m2, m2v.at[pl.ds(0, pairs2)], loc_sem.at[2]),
+        pltpu.make_async_copy(feat, feat_v.at[b], xr_sem.at[2]),
     ]
-    for n in range(3):
-        local[n].start()
     whole = pl.ds(0, slots)
     edges = (RAW, GROUP, 2 * GROUP, slots)
     first = [pl.ds(low, high - low) for low, high in zip(edges, edges[1:])]
     heads = len(first) - 1
     last = quarter - 1
-    for q in range(heads + 1):
-        own_copy(0, 0, first[q], q).start()
-
     plain = lax.broadcasted_iota(jnp.int32, (8, width), 1)
     m1v[pl.ds(pairs, 8), :] = plain
     m2v[pl.ds(pairs2, 8), :] = plain
 
     pl.semaphore_wait(barrier, 3)
-    cols_core = small(cols, col_1.at[b], 0, core)
-    cols_near = small(cols, col_2.at[s], 1, near)
+    early = pl.ds(0, RAW)
+    cols_core = small(cols, tab.at[b], 0, core)
+    cols_near = small(cols, tab.at[2], 1, near)
+    cols_across = small(cols, tab.at[3], 3, across)
     feat_core = small(feat, feat_v.at[b], 2, core)
+    raw_near = small(adj.at[2 * b + side(0), early], raw_v.at[b], 4, near)
+    raw_across = small(adj.at[2 * (1 - b) + side(0), early], raw_v.at[b], 4, across)
+    core_copy(0, 0, first[0], 0).start()
     cols_core.start()
-    for q in range(heads + 1):
-        core_copy(0, 0, first[q], q).start()
-    early = pl.ds(0, RAW)
-    raw_near = small(adj.at[2 * b + side(0), early], raw_v.at[b], 4, near)
-    raw_across = small(adj.at[2 * (1 - b) + side(0), early], raw_v.at[b], 5, across)
     raw_near.start()
     raw_across.start()
-    cols_across = small(cols, col_3, 6, across)
+    for n in range(2):
+        local[n].start()
+    own_copy(0, 0, first[0], 0).start()
+    for q in range(1, heads + 1):
+        core_copy(0, 0, first[q], q).start()
+        own_copy(0, 0, first[q], q).start()
     feat_core.start()
     cols_near.start()
     cols_across.start()
     local[3].start()
 
-    core_copy(0, 1, whole, heads + 1).start()
-    own_copy(0, 1, whole, heads + 1).start()
-
-
-    for n in range(3):
-        local[n].wait()
+    core_copy(0, 1, whole, 3).start()
+    own_copy(0, 1, whole, 3).start()
+
+
+    local[0].wait()
+    local[1].wait()
     cols_core.wait_recv()
 
     def columns(table, maps, plain_row, tile, k, bit, row):
         hots = []
         for part in range(2):
-            upper = lax.rem(table[part, k, tile] // bit, 2)
+            upper = lax.rem(tab[table[part], k, tile] // bit, 2)
             here = maps[pl.ds(upper * row + (1 - upper) * plain_row, 1), :]
             hots.append(turned(here, width))
         return jnp.concatenate(hots, axis=1)
@@ -173,9 +172,9 @@
                 continue
             hots = []
             for k in ks:
-                c = col_1[0, k, tile]
+                c = tab[b, k, tile]
                 p = c // (2 * span) * span + lax.rem(c, span)
-                hots.append(columns(col_1, m1v, pairs, tile, k, span, p))
+                hots.append(columns((0, 1), m1v, pairs, tile, k, span, p))
             done = merged(
                 [adj_v[0, j, i, k] for k in ks], [adj_v[1, j, i, k] for k in ks], rows, hots
             )
@@ -196,7 +195,7 @@
         rows = turned(m2v[pl.ds(high, 1), :], width)
         hots = []
         for k in ks:
-            c = col_2[s, k, tile]
+            c = tab[b, k, tile]
             p = c // (2 * span) * span + lax.rem(c, span)
             g = p // (2 * tiles) * tiles + lax.rem(p, tiles)
             upper = lax.rem(c // tiles, 2)
@@ -231,50 +230,53 @@
 
     @pl.loop(2, quarter)
     def _(i):
-        core_copy(0, i, whole, heads + i).start()
-        own_copy(0, i, whole, heads + i).start()
+        core_copy(0, i, whole, 4).start()
+        own_copy(0, i, whole, 4).start()
 
     @pl.loop(0, quarter)
     def _(i):
-        core_copy(1, i, whole, heads + quarter + i).start()
-        own_copy(1, i, whole, heads + quarter + i).start()
-
-    local[4].start()
-    local[3].wait()
-    feat_core.wait_recv()
+        core_copy(1, i, whole, 5).start()
+        own_copy(1, i, whole, 5).start()
+
+    local[2].start()
+    all_of(feat_v, xr_sem.at[2])
     for i in range(quarter):
         tile = 4 * i + 2 * b + side(0)
         feature_level(0, i, tile, first_rows(tile), send_f)
-    feat_near = small(send_f, lev_f.at[s], 3, near)
+    feat_near = small(send_f, lev_f.at[s], 5, near)
     feat_near.start()
 
     for i in range(1, quarter):
         if i == last:
-            local[4].wait()
-        first_level(0, i, store_send, {0: [(whole, heads + i)]})
+            local[2].wait()
+        if i == 2:
+            all_of(adj_v.at[:, 0, pl.ds(2, quarter - 2)], got_sem.at[4])
+        first_level(0, i, store_send, {0: [(whole, 3)]} if i == 1 else {})
         if i >= LAG:
             send_tile(i - LAG, RAW if i == LAG else 0)
     for i in range(quarter - LAG, quarter):
         send_tile(i, RAW if i == 0 else 0)
 
     def keep(i):
-        tile, rows = first_level(1, i, store_keep, {0: [(whole, heads + quarter + i)]})
+        tile, rows = first_level(1, i, store_keep, {})
         feature_level(1, i, tile, rows, lev_f.at[s])
 
+    all_of(adj_v.at[:, 1], got_sem.at[5])
     pl.loop(0, last)(keep)
     keep(last)
 
-    for copy in (cols_near, cols_across, raw_near, raw_across):
-        copy.wait_recv()
+    cols_near.wait_recv()
+    cols_across.wait_recv()
+    all_of(raw_v, xr_sem.at[4])
     there = 2 * b + s
     near_pair = (blk // 2 * subs + sub + 1 - 2 * s) * tiles
     near_rows = turned(m1v[pl.ds(near_pair + there, 1), :], width)
     hots = []
     for k in range(RAW):
-        c = col_2[1 - s, k, there]
+        c = tab[2, k, there]
         p = c // (2 * span) * span + lax.rem(c, span)
         mine = lax.rem(c // span, 2)
-        other = lax.rem(col_3[k, there] // span, 2)
+        other = lax.rem(tab[3, k, there] // span, 2)
         parts = []
         for upper in (b * other + (1 - b) * mine, b * mine + (1 - b) * other):
             row = upper * p + (1 - upper) * pairs
@@ -293,10 +295,10 @@
         tile = 4 * i + 2 * b + s
         rows = second_rows(tile)
         for k in range(slots):
-            c = col_2[0, k, tile]
+            c = tab[b, k, tile]
             p = c // (2 * span) * span + lax.rem(c, span)
             g = p // (2 * tiles) * tiles + lax.rem(p, tiles)
-            hots = columns(col_2, m2v, pairs2, tile, k, tiles, g)
+            hots = columns((b * (1 - s) + 2 * s, b * s + 2 * (1 - s)), m2v, pairs2, tile, k, tiles, g)
             if k == begin:
                 all_of(lev_a.at[1 - s, i, pl.ds(k, slots - k)], sr_sem.at[i])
             fin_a[i, k] = merged([lev_a[0, i, k]], [lev_a[1, i, k]], rows, [hots])[0]
@@ -362,9 +364,7 @@
         scratch_shapes=[
             pltpu.VMEM((match_one.shape[0] + 8, width), jnp.int32),
             pltpu.VMEM((match_two.shape[0] + 8, width), jnp.int32),
-            pltpu.SMEM((2, slots, tiles), jnp.int32),
-            pltpu.SMEM((2, slots, tiles), jnp.int32),
-            pltpu.SMEM((slots, tiles), jnp.int32),
+            pltpu.SMEM((4, slots, tiles), jnp.int32),
             pltpu.VMEM((2, RAW, width, width), half),
             pltpu.VMEM((2, 2, quarter, slots, width, width), half),
             pltpu.VMEM((2,) + features.shape, half),
@@ -372,11 +372,11 @@
             pltpu.VMEM((feats, quarter * width), half),
             pltpu.VMEM((2, quarter, slots, width, width), half),
             pltpu.VMEM((2, feats, quarter * width), half),
-            dma((5,)),
-            dma((2 + 2 * quarter,)),
+            dma((3,)),
+            dma((6,)),
             dma((quarter + max(LAST),)),
             dma,
-            dma((7,)),
+            dma((6,)),
         ],
         compiler_params=pltpu.CompilerParams(
             collective_id=0, has_side_effects=True, vmem_limit_bytes=VMEM_BYTES

time: 33.9 us -> 33.9 us (level)
  no operation moved by 1% of the time
where the time goes in v6:
time: 33.9 us; the launch traced here: 33.8 us
  Pallas kernels  33.1 us (98%)
  between operations  0.64 us (2%)
    pallas_call x1, Pallas kernels, per_device(): pl.pallas_call(functools.partial(kernel, span), out_shape=(pltpu.VMEM(*ti...  32.1 us
    pallas_call x1, Pallas kernels, per_device(): pl.pallas_call(put, out_shape=(jax.ShapeDtypeStruct(*tile_out), jax.Shape...  0.99 us

profile of v6, /device:TPU:8, one launch (start us, length us, event | category | flops | bytes accessed | tf_op | source)
XLA Modules:
  0.0 33.8 jit_solution(13032728490291774068)
XLA Ops:
  0.6 32.1 %coarsen.1 = (bf16[4,8,128,128]{3,2,1,0:T(8,128)(2,1)S(1)}, bf16[16,512]{1,0:T(8,128)(2,1)S(1)}) custom-call(bf16[16,2048]{1,0:T(8,128)(2,1)} %feat.1, bf16[16,8,128,128]{3,2,1,0:T(8,128)(2,1)} %adj.1, s32[8,16]{1,0:T(8,128)} %bitcast.1, s32[4096,128]{1,0:T(8,128)} %m1.1, s32[2048,128]{1,0:T(8,128)} %m2.1), custom_call_target="tpu_custom_call" | custom-call | tf_op jit(solution)/shard_map/coarsen/pallas_call | solution.py:359
  32.8 1.0 %put.1 = (bf16[4,8,128,128]{3,2,1,0:T(8,128)(2,1)}, bf16[16,512]{1,0:T(8,128)(2,1)}) custom-call(bf16[4,8,128,128]{3,2,1,0:T(8,128)(2,1)S(1)} %get-tuple-element.4.tiles, bf16[16,512]{1,0:T(8,128)(2,1)S(1)} %get-tuple-element.5.feats), custom_call_target="tpu_custom_call" | custom-call | tf_op jit(solution)/shard_map/put/pallas_call | solution.py:386

commit v7 on v6

--- a/solution.py
+++ b/solution.py
@@ -119,6 +119,13 @@
     m1v[pl.ds(pairs, 8), :] = plain
     m2v[pl.ds(pairs2, 8), :] = plain
 
+    def load_first():
+        local[1].start()
+        for q in range(heads + 1):
+            own_copy(0, 0, first[q], q).start()
+        local[0].start()
+
+    pl.when(b == 1)(load_first)
     pl.semaphore_wait(barrier, 3)
     early = pl.ds(0, RAW)
     cols_core = small(cols, tab.at[b], 0, core)
@@ -131,12 +138,9 @@
     cols_core.start()
     raw_near.start()
     raw_across.start()
-    for n in range(2):
-        local[n].start()
-    own_copy(0, 0, first[0], 0).start()
     for q in range(1, heads + 1):
         core_copy(0, 0, first[q], q).start()
-        own_copy(0, 0, first[q], q).start()
+    pl.when(b == 0)(load_first)
     feat_core.start()
     cols_near.start()
     cols_across.start()

time: 33.9 us -> 33.8 us (level)
  no operation moved by 1% of the time
where the time goes in v7:
time: 33.8 us; the launch traced here: 33.7 us
  Pallas kernels  33 us (98%)
  between operations  0.64 us (2%)
    pallas_call x1, Pallas kernels, per_device(): pl.pallas_call(functools.partial(kernel, span), out_shape=(pltpu.VMEM(*ti...  32 us
    pallas_call x1, Pallas kernels, per_device(): pl.pallas_call(put, out_shape=(jax.ShapeDtypeStruct(*tile_out), jax.Shape...  0.99 us

profile of v7, /device:TPU:8, one launch (start us, length us, event | category | flops | bytes accessed | tf_op | source)
XLA Modules:
  0.0 33.7 jit_solution(16363221888987868062)
XLA Ops:
  0.6 32.0 %coarsen.1 = (bf16[4,8,128,128]{3,2,1,0:T(8,128)(2,1)S(1)}, bf16[16,512]{1,0:T(8,128)(2,1)S(1)}) custom-call(bf16[16,2048]{1,0:T(8,128)(2,1)} %feat.1, bf16[16,8,128,128]{3,2,1,0:T(8,128)(2,1)} %adj.1, s32[8,16]{1,0:T(8,128)} %bitcast.1, s32[4096,128]{1,0:T(8,128)} %m1.1, s32[2048,128]{1,0:T(8,128)} %m2.1), custom_call_target="tpu_custom_call" | custom-call | tf_op jit(solution)/shard_map/coarsen/pallas_call | solution.py:363
  32.7 1.0 %put.1 = (bf16[4,8,128,128]{3,2,1,0:T(8,128)(2,1)}, bf16[16,512]{1,0:T(8,128)(2,1)}) custom-call(bf16[4,8,128,128]{3,2,1,0:T(8,128)(2,1)S(1)} %get-tuple-element.4.tiles, bf16[16,512]{1,0:T(8,128)(2,1)S(1)} %get-tuple-element.5.feats), custom_call_target="tpu_custom_call" | custom-call | tf_op jit(solution)/shard_map/put/pallas_call | solution.py:390

commit v8 on v7

--- a/solution.py
+++ b/solution.py
@@ -125,7 +125,12 @@
             own_copy(0, 0, first[q], q).start()
         local[0].start()
 
-    pl.when(b == 1)(load_first)
+    @pl.when(b == 1)
+    def _():
+        load_first()
+        local[3].start()
+        own_copy(0, 1, whole, 3).start()
+
     pl.semaphore_wait(barrier, 3)
     early = pl.ds(0, RAW)
     cols_core = small(cols, tab.at[b], 0, core)
@@ -144,10 +149,10 @@
     feat_core.start()
     cols_near.start()
     cols_across.start()
-    local[3].start()
+    pl.when(b == 0)(local[3].start)
 
     core_copy(0, 1, whole, 3).start()
-    own_copy(0, 1, whole, 3).start()
+    pl.when(b == 0)(own_copy(0, 1, whole, 3).start)
 
 
     local[0].wait()

time: 33.8 us -> 33.8 us (level)
  no operation moved by 1% of the time
where the time goes in v8:
time: 33.8 us; the launch traced here: 33.7 us
  Pallas kernels  33 us (98%)
  between operations  0.64 us (2%)
    pallas_call x1, Pallas kernels, per_device(): pl.pallas_call(functools.partial(kernel, span), out_shape=(pltpu.VMEM(*ti...  32 us
    pallas_call x1, Pallas kernels, per_device(): pl.pallas_call(put, out_shape=(jax.ShapeDtypeStruct(*tile_out), jax.Shape...  0.99 us

profile of v8, /device:TPU:8, one launch (start us, length us, event | category | flops | bytes accessed | tf_op | source)
XLA Modules:
  0.0 33.7 jit_solution(6325099932626869041)
XLA Ops:
  0.6 32.0 %coarsen.1 = (bf16[4,8,128,128]{3,2,1,0:T(8,128)(2,1)S(1)}, bf16[16,512]{1,0:T(8,128)(2,1)S(1)}) custom-call(bf16[16,2048]{1,0:T(8,128)(2,1)} %feat.1, bf16[16,8,128,128]{3,2,1,0:T(8,128)(2,1)} %adj.1, s32[8,16]{1,0:T(8,128)} %bitcast.1, s32[4096,128]{1,0:T(8,128)} %m1.1, s32[2048,128]{1,0:T(8,128)} %m2.1), custom_call_target="tpu_custom_call" | custom-call | tf_op jit(solution)/shard_map/coarsen/pallas_call | solution.py:368
  32.7 1.0 %put.1 = (bf16[4,8,128,128]{3,2,1,0:T(8,128)(2,1)}, bf16[16,512]{1,0:T(8,128)(2,1)}) custom-call(bf16[4,8,128,128]{3,2,1,0:T(8,128)(2,1)S(1)} %get-tuple-element.4.tiles, bf16[16,512]{1,0:T(8,128)(2,1)S(1)} %get-tuple-element.5.feats), custom_call_target="tpu_custom_call" | custom-call | tf_op jit(solution)/shard_map/put/pallas_call | solution.py:395
